TPU v7x, 512 devices: a whole 4x8x8 slice. The times are simulated.
512 devices in a mesh: energy: 64 (over z, x, core), slab: 8 (over y).
Axes of the slice: x: 4, y: 8, z: 8, core: 2. Of those that a mesh axis runs over, the one named last changes fastest.
Arguments:
- energies: float32 [64], P('energy'), may hold values from 0.6 to 1.2
- hamiltonian: float32 [8, 256, 256], P('slab')
- coupling: float32 [8, 64, 64], P('slab'), may hold values from -1.04 to 1.04
- green_prev: float32 [64, 8, 2, 256, 256], P('energy', 'slab'), may hold values from -0.5 to 0.5
- profile: float32 [256, 256], replicated, may hold values from 0.2 to 1
- phonon_weights: float32 [8], replicated, may hold values from 0.02 to 0.1
- source: int32 [64, 2], P('energy'), may hold values from 0 to 63, as said below
- weight_index: int32 [64, 2], P('energy'), may hold values from 0 to 7
- left_face: int32 [8, 64], P('slab'), may hold values from 0 to 255, as said below
- right_face: int32 [8, 64], P('slab'), may hold values from 0 to 255, as said below
Outputs:
- green: float32 [64, 8, 2, 256, 256], P('energy', 'slab')
Inputs may be any that keep to these rules, and one draw needn't show every extreme that they name: source[j, 0] = min(j + d, 63) and source[j, 1] = max(j - d', 0) with d, d' in 1 .. 5; in each column some energy has its partner exactly 5 points away. `left_face`: each row holds 64 distinct orbitals. right_face[s] holds the same 64 orbitals as left_face[s], in an order of its own.
All inputs are finite; a program needn't handle non-finite values.
Results may differ from a plain program's by a relative error of at most 0.00011.
Values sent between devices are 32-bit elements; how exact they have to be, the bound alone decides.
A program may use at most 64 MiB of HBM per device.

v0:
```python
import jax
import jax.numpy as jnp
from jax import lax
from jax.sharding import PartitionSpec as P

SPAN = 5
NEWTON = 5


BROAD = 0.02
highest = lax.Precision.HIGHEST


def passed_along(value, axis, steps):
    count = lax.axis_size(axis)
    initial, last = (max(0, -steps), min(count, count - steps))
    return lax.ppermute(value, axis, [(source, source + steps) for source in range(initial, last)])


def product(left, right):
    return jnp.matmul(left, right, precision=highest)


def complex_product(a_real, a_imag, b_real, b_imag):
    return (
        product(a_real, b_real) - product(a_imag, b_imag),
        product(a_real, b_imag) + product(a_imag, b_real),
    )


def invert(a_real, a_imag):
    width = a_real.shape[-1]
    unit = jnp.eye(width, dtype=a_real.dtype)
    modulus = jnp.sqrt(a_real * a_real + a_imag * a_imag)
    col_norm = jnp.max(jnp.sum(modulus, axis=-2), axis=-1)
    row_norm = jnp.max(jnp.sum(modulus, axis=-1), axis=-1)
    scale = (1.0 / (col_norm * row_norm))[..., None, None]
    x_real = scale * jnp.swapaxes(a_real, -1, -2)
    x_imag = -scale * jnp.swapaxes(a_imag, -1, -2)
    for turn in range(NEWTON):
        p_real, p_imag = complex_product(a_real, a_imag, x_real, x_imag)
        x_real, x_imag = complex_product(x_real, x_imag, 2.0 * unit - p_real, -p_imag)
    return (x_real, x_imag)


def corner(block, hot):
    return product(product(hot, block), hot.T)


def place(block, hot):
    return product(product(hot.T, block), hot)


def forward_step(incoming, a_real, a_imag, coup, left_hot, right_hot, first):
    faces = coup.shape[0]
    in_real = incoming[..., :faces]
    in_imag = incoming[..., faces:]
    lead = -0.5 * product(coup.T, coup)
    inner_real = product(product(coup.T, in_real), coup)
    inner_imag = product(product(coup.T, in_imag), coup)
    b_real = jnp.where(first, 0.0, inner_real)
    b_imag = jnp.where(first, lead, inner_imag)
    g_real, g_imag = invert(a_real - place(b_real, left_hot), a_imag - place(b_imag, left_hot))
    outgoing = jnp.concatenate([corner(g_real, right_hot), corner(g_imag, right_hot)], axis=-1)
    return (g_real, g_imag, outgoing)


def backward_step(incoming, g_real, g_imag, coup, left_hot, right_hot):
    faces = coup.shape[0]
    m_real = incoming[..., :faces]
    m_imag = incoming[..., faces:]
    col_real = product(g_real, right_hot.T)
    col_imag = product(g_imag, right_hot.T)
    row_real = product(right_hot, g_real)
    row_imag = product(right_hot, g_imag)
    t_real, t_imag = complex_product(col_real, col_imag, m_real, m_imag)
    c_real, c_imag = complex_product(t_real, t_imag, row_real, row_imag)
    big_real = g_real + c_real
    big_imag = g_imag + c_imag
    out_real = product(product(coup, corner(big_real, left_hot)), coup.T)
    out_imag = product(product(coup, corner(big_imag, left_hot)), coup.T)
    return (big_real, big_imag, jnp.concatenate([out_real, out_imag], axis=-1))


def on_device(
    energies,
    hamiltonian,
    coupling,
    green_prev,
    profile,
    phonon_weights,
    source,
    weight_index,
    left_face,
    right_face,
):
    count_dev = energies.shape[0]
    width = hamiltonian.shape[1]
    faces = coupling.shape[1]
    base = lax.axis_index("energy") * count_dev
    reach = (SPAN + count_dev - 1) // count_dev
    table_size = phonon_weights.shape[0]
    chosen = jnp.sum(
        phonon_weights[None, None, :]
        * (weight_index[:, :, None] == jnp.arange(table_size, dtype=jnp.int32)[None, None, :]),
        axis=2,
    )

    def add_piece(total, piece, start):
        rows = piece.shape[0]
        position = start + jnp.arange(rows, dtype=jnp.int32)
        coef = jnp.sum(chosen[:, :, None] * (source[:, :, None] == position[None, None, :]), axis=1)
        return total + product(coef, piece.reshape(rows, -1))

    summed = add_piece(jnp.zeros((count_dev, 2 * width * width), jnp.float32), green_prev, base)
    for offset in range(1, reach + 1):
        rows = count_dev
        upper = passed_along(green_prev, "energy", -offset)
        lower = passed_along(green_prev, "energy", offset)
        summed = add_piece(summed, upper, base + offset * count_dev)
        summed = add_piece(summed, lower, base - offset * count_dev + count_dev - rows)
    sigma = summed.reshape(count_dev, 2, width, width) * profile
    unit = jnp.eye(width, dtype=jnp.float32)
    a_real = energies[:, None, None] * unit - hamiltonian[0] - sigma[:, 0]
    a_imag = BROAD * unit - sigma[:, 1]
    coup = coupling[0]
    orbitals = jnp.arange(width, dtype=jnp.int32)
    left_hot = (left_face[0][:, None] == orbitals[None, :]).astype(jnp.float32)
    right_hot = (right_face[0][:, None] == orbitals[None, :]).astype(jnp.float32)
    slab_index = lax.axis_index("slab")
    slab_count = lax.axis_size("slab")
    first = slab_index == 0
    blocks = jnp.zeros((count_dev, width, width), jnp.float32)
    face_zero = jnp.zeros((count_dev, faces, 2 * faces), jnp.float32)

    def forward_turn(section, carry):
        g_real, g_imag, sent = carry
        incoming = passed_along(sent, "slab", 1)

        def forward_work(operand):
            return forward_step(operand, a_real, a_imag, coup, left_hot, right_hot, first)

        def forward_keep(operand):
            return (g_real, g_imag, sent)

        return lax.cond(slab_index == section, forward_work, forward_keep, incoming)

    g_real, g_imag, sent = lax.fori_loop(0, slab_count, forward_turn, (blocks, blocks, face_zero))

    def backward_turn(section, carry):
        big_real, big_imag, sent = carry
        incoming = passed_along(sent, "slab", -1)

        def backward_work(operand):
            return backward_step(operand, g_real, g_imag, coup, left_hot, right_hot)

        def backward_keep(operand):
            return (big_real, big_imag, sent)

        return lax.cond(
            slab_index == slab_count - 1 - section, backward_work, backward_keep, incoming
        )

    big_real, big_imag, sent = lax.fori_loop(
        0, slab_count, backward_turn, (blocks, blocks, face_zero)
    )
    return jnp.stack([big_real, big_imag], axis=1)[:, None]


def solution(mesh):
    in_specs = (
        P("energy"),
        P("slab", None, None),
        P("slab", None, None),
        P("energy", "slab", None, None, None),
        P(),
        P(),
        P("energy", None),
        P("energy", None),
        P("slab", None),
        P("slab", None),
    )
    out_specs = P("energy", "slab", None, None, None)
    return jax.shard_map(
        on_device, mesh=mesh, in_specs=in_specs, out_specs=out_specs, check_vma=False
    )
```

profile of v0, /device:TPU:6, one launch (start us, length us, event | category | flops | bytes accessed | tf_op | source)
XLA Modules:
  0.0 474.0 jit_solution(627379610311913728)
XLA Ops:
  0.0 1.9 collective-permute-start.10
  1.9 6.0 %collective-permute-start.11 = (f32[1,1,2,256,256]{4,3,2,1,0:T(8,128)}, f32[1,1,2,256,256]{4,3,2,1,0:T(8,128)S(1)}, u32[]{:S(2)}, u32[]{:S(2)}) collective-permute-start(f32[1,1,2,256,256]{4,3,2,1,0:T(8,128)} %param.21), channel_id=1, source_target_pairs={{0,40},{8,48},{16,56},{24,64},{32,72},{40,80},{48,88},{56,96},{64,... | collective-permute-start | bytes 1572872 | tf_op jit(solution)/shard_map/ppermute | solution.py:17
  8.0 4.2 collective-permute-start.2
  12.2 1.9 collective-permute-start.3
  14.1 2.3 collective-permute-start.4
  16.4 2.8 collective-permute-done.10
  19.2 12.4 %collective-permute-start.5 = (f32[1,1,2,256,256]{4,3,2,1,0:T(8,128)}, f32[1,1,2,256,256]{4,3,2,1,0:T(8,128)S(1)}, u32[]{:S(2)}, u32[]{:S(2)}) collective-permute-start(f32[1,1,2,256,256]{4,3,2,1,0:T(8,128)} %param.21), channel_id=1, source_target_pairs={{0,16},{8,24},{16,32},{24,40},{32,48},{40,56},{48,64},{56,72},{64,... | collective-permute-start | bytes 1572872 | tf_op jit(solution)/shard_map/ppermute | solution.py:17
  31.6 15.6 %collective-permute-done.11 = f32[1,1,2,256,256]{4,3,2,1,0:T(8,128)S(1)} collective-permute-done((f32[1,1,2,256,256]{4,3,2,1,0:T(8,128)}, f32[1,1,2,256,256]{4,3,2,1,0:T(8,128)S(1)}, u32[]{:S(2)}, u32[]{:S(2)}) %collective-permute-start.11) | collective-permute-done | bytes 524320 | tf_op jit(solution)/shard_map/ppermute | solution.py:17
  47.2 1.9 collective-permute-start.6
  49.1 5.8 %collective-permute-start.7 = (f32[1,1,2,256,256]{4,3,2,1,0:T(8,128)}, f32[1,1,2,256,256]{4,3,2,1,0:T(8,128)}, u32[]{:S(2)}, u32[]{:S(2)}) collective-permute-start(f32[1,1,2,256,256]{4,3,2,1,0:T(8,128)} %param.21), channel_id=1, source_target_pairs={{0,24},{8,32},{16,40},{24,48},{32,56},{40,64},{48,72},{56,80},{64,... | collective-permute-start | bytes 1572872 | tf_op jit(solution)/shard_map/ppermute | solution.py:17
  54.9 1.9 collective-permute-start.8
  56.8 7.6 %collective-permute-start.9 = (f32[1,1,2,256,256]{4,3,2,1,0:T(8,128)}, f32[1,1,2,256,256]{4,3,2,1,0:T(8,128)}, u32[]{:S(2)}, u32[]{:S(2)}) collective-permute-start(f32[1,1,2,256,256]{4,3,2,1,0:T(8,128)} %param.21), channel_id=1, source_target_pairs={{0,32},{8,40},{16,48},{24,56},{32,64},{40,72},{48,80},{56,88},{64,... | collective-permute-start | bytes 1572872 | tf_op jit(solution)/shard_map/ppermute | solution.py:17
  65.1 0.6 copy-done.9
  66.4 0.7 fusion.117
  67.1 12.9 %collective-permute-done.7 = f32[1,1,2,256,256]{4,3,2,1,0:T(8,128)} collective-permute-done((f32[1,1,2,256,256]{4,3,2,1,0:T(8,128)}, f32[1,1,2,256,256]{4,3,2,1,0:T(8,128)}, u32[]{:S(2)}, u32[]{:S(2)}) %collective-permute-start.7) | collective-permute-done | bytes 524320 | tf_op jit(solution)/shard_map/ppermute | solution.py:17
  80.1 5.0 %collective-permute-done.9 = f32[1,1,2,256,256]{4,3,2,1,0:T(8,128)} collective-permute-done((f32[1,1,2,256,256]{4,3,2,1,0:T(8,128)}, f32[1,1,2,256,256]{4,3,2,1,0:T(8,128)}, u32[]{:S(2)}, u32[]{:S(2)}) %collective-permute-start.9) | collective-permute-done | bytes 524320 | tf_op jit(solution)/shard_map/ppermute | solution.py:17
  85.1 9.1 %bitcast_multiply_fusion = f32[1,2,256,256]{3,2,1,0:T(8,128)S(1)} fusion(f32[1,1,2,256,256]{4,3,2,1,0:T(8,128)S(1)} %collective-permute-done.11, f32[1,1,2,256,256]{4,3,2,1,0:T(8,128)S(1)} %collective-permute-done.10, f32[1,1,2,256,256]{4,3,2,1,0:T(8,128)} %collective-permute-done.9, f32[1,1,2,256,256]{4,3,2,1,0:T(8,128)} %collective-permute-done.8, ...), kind=kLoop, calls=%fused_computation.152 | loop fusion | flops 2883584 | bytes 6553644 | tf_op jit(solution)/shard_map/mul | solution.py:122
  94.3 0.7 broadcast_in_dim.10.clone.1
  95.8 141.7 %while.36 = (s32[]{:T(128)}, f32[1,256,256]{2,1,0:T(8,128)}, f32[1,256,256]{2,1,0:T(8,128)S(1)}, f32[1,64,128]{2,1,0:T(8,128)S(1)}, s32[]{:T(128)}, /*index=5*/p...) while((s32[]{:T(128)}, f32[1,256,256]{2,1,0:T(8,128)}, ...), condition=%wide.region_19.20_spmd.clone, body=%wide.region_12.19_spmd.clone.sunk | while | flops 8324141056 | bytes 41833376 | solution.py:148
  95.8 3.5 collective-permute-start
  99.4 1.5 collective-permute-done
  100.9 25.9 %conditional.6 = ((f32[1,256,256]{2,1,0:T(8,128)}, f32[1,256,256]{2,1,0:T(8,128)S(1)}, f32[1,64,128]{2,1,0:T(8,128)S(1)})) conditional(s32[]{:T(128)} %convert_element_type.64, (f32[1,256,256]{2,1,0:T(8,128)}, f32[1,256,256]{2,1,0:T(8,128)S(1)}, f32[1,64,128]{2,1,0:T(8,128)S(1)}) %tuple.96, (pred[]{:T(512)}, f32[1,64,128]{2,1,0:T(8,128)S(1)}, ...), branch_computations={%region_13.0_spmd, %region_14.18_spmd} | conditional | flops 8324075520 | bytes 41570472 | solution.py:146
  103.5 0.7 reduce_max.16
  108.3 0.6 convolution_add_fusion.8
  123.2 1.1 convolution_subtract_fusion
  124.3 1.5 fusion.138
  126.7 1.3 collective-permute-start
  128.1 1.5 collective-permute-done
  129.6 30.1 %collective-permute-start = (f32[1,64,128]{2,1,0:T(8,128)S(1)}, f32[1,64,128]{2,1,0:T(8,128)S(1)}, u32[]{:S(2)}, u32[]{:S(2)}) collective-permute-start(f32[1,64,128]{2,1,0:T(8,128)S(1)} %get-tuple-element.728), channel_id=1, source_target_pairs={{0,1},{1,2},{2,3},{3,4},{4,5},{5,6},{6,7},{8,9},{9,10},{10,11},{11... | collective-permute-start | bytes 98312 | tf_op jit(solution)/shard_map/while/body/eval_jaxpr/ppermute | solution.py:17
  159.8 1.5 collective-permute-done
  161.3 4.3 collective-permute-start
  165.7 1.5 collective-permute-done
  167.2 27.7 %collective-permute-start = (f32[1,64,128]{2,1,0:T(8,128)S(1)}, f32[1,64,128]{2,1,0:T(8,128)S(1)}, u32[]{:S(2)}, u32[]{:S(2)}) collective-permute-start(f32[1,64,128]{2,1,0:T(8,128)S(1)} %get-tuple-element.728), channel_id=1, source_target_pairs={{0,1},{1,2},{2,3},{3,4},{4,5},{5,6},{6,7},{8,9},{9,10},{10,11},{11... | collective-permute-start | bytes 98312 | tf_op jit(solution)/shard_map/while/body/eval_jaxpr/ppermute | solution.py:17
  195.0 1.5 collective-permute-done
  196.5 4.2 collective-permute-start
  200.8 1.5 collective-permute-done
  202.3 27.8 %collective-permute-start = (f32[1,64,128]{2,1,0:T(8,128)S(1)}, f32[1,64,128]{2,1,0:T(8,128)S(1)}, u32[]{:S(2)}, u32[]{:S(2)}) collective-permute-start(f32[1,64,128]{2,1,0:T(8,128)S(1)} %get-tuple-element.728), channel_id=1, source_target_pairs={{0,1},{1,2},{2,3},{3,4},{4,5},{5,6},{6,7},{8,9},{9,10},{10,11},{11... | collective-permute-start | bytes 98312 | tf_op jit(solution)/shard_map/while/body/eval_jaxpr/ppermute | solution.py:17
  230.2 1.5 collective-permute-done
  231.7 4.2 collective-permute-start
  236.0 1.5 collective-permute-done
  237.5 0.7 broadcast_in_dim.10
  238.2 233.9 %while.37 = (s32[]{:T(128)}, f32[1,256,256]{2,1,0:T(8,128)}, f32[1,256,256]{2,1,0:T(8,128)S(1)}, f32[1,64,128]{2,1,0:T(8,128)S(1)}, s32[]{:T(128)}, /*index=5*/f...) while((s32[]{:T(128)}, f32[1,256,256]{2,1,0:T(8,128)}, ...), condition=%wide.region_23.24_spmd.clone, body=%wide.region_20.23_spmd.clone.sunk | while | flops 591765504 | bytes 8684375 | solution.py:164
  238.2 1.3 collective-permute-start.1
  239.6 29.5 %collective-permute-done.1 = f32[1,64,128]{2,1,0:T(8,128)S(1)} collective-permute-done((f32[1,64,128]{2,1,0:T(8,128)S(1)}, f32[1,64,128]{2,1,0:T(8,128)S(1)}, u32[]{:S(2)}, u32[]{:S(2)}) %collective-permute-start.1) | collective-permute-done | bytes 32800 | tf_op jit(solution)/shard_map/while/body/eval_jaxpr/ppermute | solution.py:17
  269.2 1.3 collective-permute-start.1
  270.5 5.9 %collective-permute-done.1 = f32[1,64,128]{2,1,0:T(8,128)S(1)} collective-permute-done((f32[1,64,128]{2,1,0:T(8,128)S(1)}, f32[1,64,128]{2,1,0:T(8,128)S(1)}, u32[]{:S(2)}, u32[]{:S(2)}) %collective-permute-start.1) | collective-permute-done | bytes 32800 | tf_op jit(solution)/shard_map/while/body/eval_jaxpr/ppermute | solution.py:17
  276.5 1.3 collective-permute-start.1
  277.9 27.2 %collective-permute-done.1 = f32[1,64,128]{2,1,0:T(8,128)S(1)} collective-permute-done((f32[1,64,128]{2,1,0:T(8,128)S(1)}, f32[1,64,128]{2,1,0:T(8,128)S(1)}, u32[]{:S(2)}, u32[]{:S(2)}) %collective-permute-start.1) | collective-permute-done | bytes 32800 | tf_op jit(solution)/shard_map/while/body/eval_jaxpr/ppermute | solution.py:17
  305.0 1.3 collective-permute-start.1
  306.4 5.8 %collective-permute-done.1 = f32[1,64,128]{2,1,0:T(8,128)S(1)} collective-permute-done((f32[1,64,128]{2,1,0:T(8,128)S(1)}, f32[1,64,128]{2,1,0:T(8,128)S(1)}, u32[]{:S(2)}, u32[]{:S(2)}) %collective-permute-start.1) | collective-permute-done | bytes 32800 | tf_op jit(solution)/shard_map/while/body/eval_jaxpr/ppermute | solution.py:17
  312.3 1.3 collective-permute-start.1
  313.6 27.3 %collective-permute-done.1 = f32[1,64,128]{2,1,0:T(8,128)S(1)} collective-permute-done((f32[1,64,128]{2,1,0:T(8,128)S(1)}, f32[1,64,128]{2,1,0:T(8,128)S(1)}, u32[]{:S(2)}, u32[]{:S(2)}) %collective-permute-start.1) | collective-permute-done | bytes 32800 | tf_op jit(solution)/shard_map/while/body/eval_jaxpr/ppermute | solution.py:17
  341.0 1.3 collective-permute-start.1
  342.3 5.6 %collective-permute-done.1 = f32[1,64,128]{2,1,0:T(8,128)S(1)} collective-permute-done((f32[1,64,128]{2,1,0:T(8,128)S(1)}, f32[1,64,128]{2,1,0:T(8,128)S(1)}, u32[]{:S(2)}, u32[]{:S(2)}) %collective-permute-start.1) | collective-permute-done | bytes 32800 | tf_op jit(solution)/shard_map/while/body/eval_jaxpr/ppermute | solution.py:17
  348.0 1.3 collective-permute-start.1
  349.4 26.5 %collective-permute-done.1 = f32[1,64,128]{2,1,0:T(8,128)S(1)} collective-permute-done((f32[1,64,128]{2,1,0:T(8,128)S(1)}, f32[1,64,128]{2,1,0:T(8,128)S(1)}, u32[]{:S(2)}, u32[]{:S(2)}) %collective-permute-start.1) | collective-permute-done | bytes 32800 | tf_op jit(solution)/shard_map/while/body/eval_jaxpr/ppermute | solution.py:17
  375.9 1.3 collective-permute-start.1
  377.3 83.2 %collective-permute-done.1 = f32[1,64,128]{2,1,0:T(8,128)S(1)} collective-permute-done((f32[1,64,128]{2,1,0:T(8,128)S(1)}, f32[1,64,128]{2,1,0:T(8,128)S(1)}, u32[]{:S(2)}, u32[]{:S(2)}) %collective-permute-start.1) | collective-permute-done | bytes 32800 | tf_op jit(solution)/shard_map/while/body/eval_jaxpr/ppermute | solution.py:17
  460.5 11.7 %conditional.7 = ((f32[1,256,256]{2,1,0:T(8,128)}, f32[1,256,256]{2,1,0:T(8,128)S(1)}, f32[1,64,128]{2,1,0:T(8,128)S(1)})) conditional(s32[]{:T(128)} %convert_element_type.66, (f32[1,256,256]{2,1,0:T(8,128)}, f32[1,256,256]{2,1,0:T(8,128)S(1)}, f32[1,64,128]{2,1,0:T(8,128)S(1)}) %tuple.100, (f32[1,256,256]{2,1,0:T(8,128)}, ...), branch_computations={%region_21.21_spmd, %region_22.22_spmd} | conditional | flops 591699968 | bytes 8421464 | solution.py:160
  460.5 1.3 fusion.98
  464.1 1.2 fusion.96
  467.6 2.1 fusion.86
  469.7 1.5 fusion.90
  472.2 1.8 maximum_bitcast_fusion
  (132 shorter events, 28.5 us)
Async XLA Ops:
  0.0 19.2 %collective-permute-start.10 = (f32[1,1,2,256,256]{4,3,2,1,0:T(8,128)}, f32[1,1,2,256,256]{4,3,2,1,0:T(8,128)S(1)}, u32[]{:S(2)}, u32[]{:S(2)}) collective-permute-start(f32[1,1,2,256,256]{4,3,2,1,0:T(8,128)} %param.21), channel_id=1, source_target_pairs={{40,0},{48,8},{56,16},{64,24},{72,32},{80,40},{88,48},{96,56},{104... | collective-permute-start | bytes 1572872 | tf_op jit(solution)/shard_map/ppermute | solution.py:17
  1.9 45.3 %collective-permute-start.11 = (f32[1,1,2,256,256]{4,3,2,1,0:T(8,128)}, f32[1,1,2,256,256]{4,3,2,1,0:T(8,128)S(1)}, u32[]{:S(2)}, u32[]{:S(2)}) collective-permute-start(f32[1,1,2,256,256]{4,3,2,1,0:T(8,128)} %param.21), channel_id=1, source_target_pairs={{0,40},{8,48},{16,56},{24,64},{32,72},{40,80},{48,88},{56,96},{64,... | collective-permute-start | bytes 1572872 | tf_op jit(solution)/shard_map/ppermute | solution.py:17
  8.0 41.1 %collective-permute-start.2 = (f32[1,1,2,256,256]{4,3,2,1,0:T(8,128)}, f32[1,1,2,256,256]{4,3,2,1,0:T(8,128)S(1)}, u32[]{:S(2)}, u32[]{:S(2)}) collective-permute-start(f32[1,1,2,256,256]{4,3,2,1,0:T(8,128)} %param.21), channel_id=1, source_target_pairs={{8,0},{16,8},{24,16},{32,24},{40,32},{48,40},{56,48},{64,56},{72,6... | collective-permute-start | bytes 1572872 | tf_op jit(solution)/shard_map/ppermute | solution.py:17
  12.2 42.7 %collective-permute-start.3 = (f32[1,1,2,256,256]{4,3,2,1,0:T(8,128)}, f32[1,1,2,256,256]{4,3,2,1,0:T(8,128)S(1)}, u32[]{:S(2)}, u32[]{:S(2)}) collective-permute-start(f32[1,1,2,256,256]{4,3,2,1,0:T(8,128)} %param.21), channel_id=1, source_target_pairs={{0,8},{8,16},{16,24},{24,32},{32,40},{40,48},{48,56},{56,64},{64,7... | collective-permute-start | bytes 1572872 | tf_op jit(solution)/shard_map/ppermute | solution.py:17
  14.1 42.7 %collective-permute-start.4 = (f32[1,1,2,256,256]{4,3,2,1,0:T(8,128)}, f32[1,1,2,256,256]{4,3,2,1,0:T(8,128)S(1)}, u32[]{:S(2)}, u32[]{:S(2)}) collective-permute-start(f32[1,1,2,256,256]{4,3,2,1,0:T(8,128)} %param.21), channel_id=1, source_target_pairs={{16,0},{24,8},{32,16},{40,24},{48,32},{56,40},{64,48},{72,56},{80,... | collective-permute-start | bytes 1572872 | tf_op jit(solution)/shard_map/ppermute | solution.py:17
  19.2 47.9 %collective-permute-start.5 = (f32[1,1,2,256,256]{4,3,2,1,0:T(8,128)}, f32[1,1,2,256,256]{4,3,2,1,0:T(8,128)S(1)}, u32[]{:S(2)}, u32[]{:S(2)}) collective-permute-start(f32[1,1,2,256,256]{4,3,2,1,0:T(8,128)} %param.21), channel_id=1, source_target_pairs={{0,16},{8,24},{16,32},{24,40},{32,48},{40,56},{48,64},{56,72},{64,... | collective-permute-start | bytes 1572872 | tf_op jit(solution)/shard_map/ppermute | solution.py:17
  47.2 19.9 %collective-permute-start.6 = (f32[1,1,2,256,256]{4,3,2,1,0:T(8,128)}, f32[1,1,2,256,256]{4,3,2,1,0:T(8,128)}, u32[]{:S(2)}, u32[]{:S(2)}) collective-permute-start(f32[1,1,2,256,256]{4,3,2,1,0:T(8,128)} %param.21), channel_id=1, source_target_pairs={{24,0},{32,8},{40,16},{48,24},{56,32},{64,40},{72,48},{80,56},{88,... | collective-permute-start | bytes 1572872 | tf_op jit(solution)/shard_map/ppermute | solution.py:17
  49.1 30.9 %collective-permute-start.7 = (f32[1,1,2,256,256]{4,3,2,1,0:T(8,128)}, f32[1,1,2,256,256]{4,3,2,1,0:T(8,128)}, u32[]{:S(2)}, u32[]{:S(2)}) collective-permute-start(f32[1,1,2,256,256]{4,3,2,1,0:T(8,128)} %param.21), channel_id=1, source_target_pairs={{0,24},{8,32},{16,40},{24,48},{32,56},{40,64},{48,72},{56,80},{64,... | collective-permute-start | bytes 1572872 | tf_op jit(solution)/shard_map/ppermute | solution.py:17
  54.9 25.2 %collective-permute-start.8 = (f32[1,1,2,256,256]{4,3,2,1,0:T(8,128)}, f32[1,1,2,256,256]{4,3,2,1,0:T(8,128)}, u32[]{:S(2)}, u32[]{:S(2)}) collective-permute-start(f32[1,1,2,256,256]{4,3,2,1,0:T(8,128)} %param.21), channel_id=1, source_target_pairs={{32,0},{40,8},{48,16},{56,24},{64,32},{72,40},{80,48},{88,56},{96,... | collective-permute-start | bytes 1572872 | tf_op jit(solution)/shard_map/ppermute | solution.py:17
  56.8 28.2 %collective-permute-start.9 = (f32[1,1,2,256,256]{4,3,2,1,0:T(8,128)}, f32[1,1,2,256,256]{4,3,2,1,0:T(8,128)}, u32[]{:S(2)}, u32[]{:S(2)}) collective-permute-start(f32[1,1,2,256,256]{4,3,2,1,0:T(8,128)} %param.21), channel_id=1, source_target_pairs={{0,32},{8,40},{16,48},{24,56},{32,64},{40,72},{48,80},{56,88},{64,... | collective-permute-start | bytes 1572872 | tf_op jit(solution)/shard_map/ppermute | solution.py:17
  65.1 0.7 copy-start.9
  65.1 0.7 copy-start.10
  65.8 0.7 copy-start.8
  85.1 9.1 %copy-start.5 = (f32[1,256,256]{2,1,0:T(8,128)S(1)}, f32[1,256,256]{2,1,0:T(8,128)}, u32[]{:S(2)}) copy-start(f32[1,256,256]{2,1,0:T(8,128)} %param.19) | copy-start | bytes 786436
  95.0 0.7 copy-start.7
  95.0 0.8 copy-start.2
  95.0 0.8 copy-start.6
  95.8 5.1 %collective-permute-start = (f32[1,64,128]{2,1,0:T(8,128)S(1)}, f32[1,64,128]{2,1,0:T(8,128)S(1)}, u32[]{:S(2)}, u32[]{:S(2)}) collective-permute-start(f32[1,64,128]{2,1,0:T(8,128)S(1)} %get-tuple-element.728), channel_id=1, source_target_pairs={{0,1},{1,2},{2,3},{3,4},{4,5},{5,6},{6,7},{8,9},{9,10},{10,11},{11... | collective-permute-start | bytes 98312 | tf_op jit(solution)/shard_map/while/body/eval_jaxpr/ppermute | solution.py:17
  121.8 1.0 copy-start
  125.8 1.0 copy-start.1
  126.7 2.9 collective-permute-start
  129.6 31.7 %collective-permute-start = (f32[1,64,128]{2,1,0:T(8,128)S(1)}, f32[1,64,128]{2,1,0:T(8,128)S(1)}, u32[]{:S(2)}, u32[]{:S(2)}) collective-permute-start(f32[1,64,128]{2,1,0:T(8,128)S(1)} %get-tuple-element.728), channel_id=1, source_target_pairs={{0,1},{1,2},{2,3},{3,4},{4,5},{5,6},{6,7},{8,9},{9,10},{10,11},{11... | collective-permute-start | bytes 98312 | tf_op jit(solution)/shard_map/while/body/eval_jaxpr/ppermute | solution.py:17
  161.3 5.9 %collective-permute-start = (f32[1,64,128]{2,1,0:T(8,128)S(1)}, f32[1,64,128]{2,1,0:T(8,128)S(1)}, u32[]{:S(2)}, u32[]{:S(2)}) collective-permute-start(f32[1,64,128]{2,1,0:T(8,128)S(1)} %get-tuple-element.728), channel_id=1, source_target_pairs={{0,1},{1,2},{2,3},{3,4},{4,5},{5,6},{6,7},{8,9},{9,10},{10,11},{11... | collective-permute-start | bytes 98312 | tf_op jit(solution)/shard_map/while/body/eval_jaxpr/ppermute | solution.py:17
  167.2 29.3 %collective-permute-start = (f32[1,64,128]{2,1,0:T(8,128)S(1)}, f32[1,64,128]{2,1,0:T(8,128)S(1)}, u32[]{:S(2)}, u32[]{:S(2)}) collective-permute-start(f32[1,64,128]{2,1,0:T(8,128)S(1)} %get-tuple-element.728), channel_id=1, source_target_pairs={{0,1},{1,2},{2,3},{3,4},{4,5},{5,6},{6,7},{8,9},{9,10},{10,11},{11... | collective-permute-start | bytes 98312 | tf_op jit(solution)/shard_map/while/body/eval_jaxpr/ppermute | solution.py:17
  196.5 5.8 %collective-permute-start = (f32[1,64,128]{2,1,0:T(8,128)S(1)}, f32[1,64,128]{2,1,0:T(8,128)S(1)}, u32[]{:S(2)}, u32[]{:S(2)}) collective-permute-start(f32[1,64,128]{2,1,0:T(8,128)S(1)} %get-tuple-element.728), channel_id=1, source_target_pairs={{0,1},{1,2},{2,3},{3,4},{4,5},{5,6},{6,7},{8,9},{9,10},{10,11},{11... | collective-permute-start | bytes 98312 | tf_op jit(solution)/shard_map/while/body/eval_jaxpr/ppermute | solution.py:17
  202.3 29.4 %collective-permute-start = (f32[1,64,128]{2,1,0:T(8,128)S(1)}, f32[1,64,128]{2,1,0:T(8,128)S(1)}, u32[]{:S(2)}, u32[]{:S(2)}) collective-permute-start(f32[1,64,128]{2,1,0:T(8,128)S(1)} %get-tuple-element.728), channel_id=1, source_target_pairs={{0,1},{1,2},{2,3},{3,4},{4,5},{5,6},{6,7},{8,9},{9,10},{10,11},{11... | collective-permute-start | bytes 98312 | tf_op jit(solution)/shard_map/while/body/eval_jaxpr/ppermute | solution.py:17
  231.7 5.8 %collective-permute-start = (f32[1,64,128]{2,1,0:T(8,128)S(1)}, f32[1,64,128]{2,1,0:T(8,128)S(1)}, u32[]{:S(2)}, u32[]{:S(2)}) collective-permute-start(f32[1,64,128]{2,1,0:T(8,128)S(1)} %get-tuple-element.728), channel_id=1, source_target_pairs={{0,1},{1,2},{2,3},{3,4},{4,5},{5,6},{6,7},{8,9},{9,10},{10,11},{11... | collective-permute-start | bytes 98312 | tf_op jit(solution)/shard_map/while/body/eval_jaxpr/ppermute | solution.py:17
  238.2 30.9 %collective-permute-start.1 = (f32[1,64,128]{2,1,0:T(8,128)S(1)}, f32[1,64,128]{2,1,0:T(8,128)S(1)}, u32[]{:S(2)}, u32[]{:S(2)}) collective-permute-start(f32[1,64,128]{2,1,0:T(8,128)S(1)} %get-tuple-element.764), channel_id=1, source_target_pairs={{1,0},{2,1},{3,2},{4,3},{5,4},{6,5},{7,6},{9,8},{10,9},{11,10},{12... | collective-permute-start | bytes 98312 | tf_op jit(solution)/shard_map/while/body/eval_jaxpr/ppermute | solution.py:17
  269.2 7.3 %collective-permute-start.1 = (f32[1,64,128]{2,1,0:T(8,128)S(1)}, f32[1,64,128]{2,1,0:T(8,128)S(1)}, u32[]{:S(2)}, u32[]{:S(2)}) collective-permute-start(f32[1,64,128]{2,1,0:T(8,128)S(1)} %get-tuple-element.764), channel_id=1, source_target_pairs={{1,0},{2,1},{3,2},{4,3},{5,4},{6,5},{7,6},{9,8},{10,9},{11,10},{12... | collective-permute-start | bytes 98312 | tf_op jit(solution)/shard_map/while/body/eval_jaxpr/ppermute | solution.py:17
  276.5 28.6 %collective-permute-start.1 = (f32[1,64,128]{2,1,0:T(8,128)S(1)}, f32[1,64,128]{2,1,0:T(8,128)S(1)}, u32[]{:S(2)}, u32[]{:S(2)}) collective-permute-start(f32[1,64,128]{2,1,0:T(8,128)S(1)} %get-tuple-element.764), channel_id=1, source_target_pairs={{1,0},{2,1},{3,2},{4,3},{5,4},{6,5},{7,6},{9,8},{10,9},{11,10},{12... | collective-permute-start | bytes 98312 | tf_op jit(solution)/shard_map/while/body/eval_jaxpr/ppermute | solution.py:17
  305.0 7.2 %collective-permute-start.1 = (f32[1,64,128]{2,1,0:T(8,128)S(1)}, f32[1,64,128]{2,1,0:T(8,128)S(1)}, u32[]{:S(2)}, u32[]{:S(2)}) collective-permute-start(f32[1,64,128]{2,1,0:T(8,128)S(1)} %get-tuple-element.764), channel_id=1, source_target_pairs={{1,0},{2,1},{3,2},{4,3},{5,4},{6,5},{7,6},{9,8},{10,9},{11,10},{12... | collective-permute-start | bytes 98312 | tf_op jit(solution)/shard_map/while/body/eval_jaxpr/ppermute | solution.py:17
  312.3 28.7 %collective-permute-start.1 = (f32[1,64,128]{2,1,0:T(8,128)S(1)}, f32[1,64,128]{2,1,0:T(8,128)S(1)}, u32[]{:S(2)}, u32[]{:S(2)}) collective-permute-start(f32[1,64,128]{2,1,0:T(8,128)S(1)} %get-tuple-element.764), channel_id=1, source_target_pairs={{1,0},{2,1},{3,2},{4,3},{5,4},{6,5},{7,6},{9,8},{10,9},{11,10},{12... | collective-permute-start | bytes 98312 | tf_op jit(solution)/shard_map/while/body/eval_jaxpr/ppermute | solution.py:17
  341.0 7.0 %collective-permute-start.1 = (f32[1,64,128]{2,1,0:T(8,128)S(1)}, f32[1,64,128]{2,1,0:T(8,128)S(1)}, u32[]{:S(2)}, u32[]{:S(2)}) collective-permute-start(f32[1,64,128]{2,1,0:T(8,128)S(1)} %get-tuple-element.764), channel_id=1, source_target_pairs={{1,0},{2,1},{3,2},{4,3},{5,4},{6,5},{7,6},{9,8},{10,9},{11,10},{12... | collective-permute-start | bytes 98312 | tf_op jit(solution)/shard_map/while/body/eval_jaxpr/ppermute | solution.py:17
  348.0 27.9 %collective-permute-start.1 = (f32[1,64,128]{2,1,0:T(8,128)S(1)}, f32[1,64,128]{2,1,0:T(8,128)S(1)}, u32[]{:S(2)}, u32[]{:S(2)}) collective-permute-start(f32[1,64,128]{2,1,0:T(8,128)S(1)} %get-tuple-element.764), channel_id=1, source_target_pairs={{1,0},{2,1},{3,2},{4,3},{5,4},{6,5},{7,6},{9,8},{10,9},{11,10},{12... | collective-permute-start | bytes 98312 | tf_op jit(solution)/shard_map/while/body/eval_jaxpr/ppermute | solution.py:17
  375.9 84.6 %collective-permute-start.1 = (f32[1,64,128]{2,1,0:T(8,128)S(1)}, f32[1,64,128]{2,1,0:T(8,128)S(1)}, u32[]{:S(2)}, u32[]{:S(2)}) collective-permute-start(f32[1,64,128]{2,1,0:T(8,128)S(1)} %get-tuple-element.764), channel_id=1, source_target_pairs={{1,0},{2,1},{3,2},{4,3},{5,4},{6,5},{7,6},{9,8},{10,9},{11,10},{12... | collective-permute-start | bytes 98312 | tf_op jit(solution)/shard_map/while/body/eval_jaxpr/ppermute | solution.py:17
  465.7 1.0 copy-start.3
  471.2 1.0 copy-start.4
where the time goes:
time: 482 us; the launch traced here: 474 us
  waiting for transfers between devices  259 us (54%)
  starting transfers between devices  159 us (33%)
  matrix products  33.8 us (7%)
  other arithmetic  14.6 us (3%)
    ppermute x26, waiting for transfers between devices, passed_along(): lax.ppermute(value, axis, [(source, source + steps) for source in range(i...  259 us
    ppermute x26, starting transfers between devices, passed_along(): lax.ppermute(value, axis, [(source, source + steps) for source in range(i...  159 us
    dot_general x73, matrix products, product(): return jnp.matmul(left, right, precision=highest)  33.8 us
  transfers between devices with their start and end apart: 26, of which 20 were waited for; matrix products, arithmetic and copies ran while one was open for 0% of the time, Pallas kernels for 0%

commit v1 on v0

v1 whole, which is shorter than its diff:
```python
import functools
import jax
import jax.numpy as jnp
from jax import lax
from jax.experimental import pallas as pl
from jax.experimental.pallas import tpu as pltpu
from jax.sharding import PartitionSpec as P

SPAN = 5
BROAD = 0.02
f32 = jnp.float32
bf16 = jnp.bfloat16
MESH = pl.DeviceIdType.MESH
highest = lax.Precision.HIGHEST


def mm(left, right):
    return jnp.dot(left, right, preferred_element_type=f32)


def mmt(left, right):
    return lax.dot_general(left, right, (((1,), (1,)), ((), ())), preferred_element_type=f32)


def split(value):
    high = value.astype(bf16)
    return high, (value - high.astype(f32)).astype(bf16)


def lanes(*pieces):
    return jnp.concatenate(pieces, axis=1)


def rows(*pieces):
    return jnp.concatenate(pieces, axis=0)


def left3(value):
    high, low = split(value)
    return lanes(high, high, low)


def right3(value):
    high, low = split(value)
    return lanes(high, low, high)


def right3v(value):
    high, low = split(value)
    return rows(high, low, high)


def swapped(packed, low_sign, high_sign):
    half = packed.shape[1] // 2
    lane = lax.broadcasted_iota(jnp.int32, packed.shape, 1)
    turned = lanes(packed[:, half:], packed[:, :half])
    return jnp.where(lane < half, low_sign * turned, high_sign * turned)


def as_right(packed):
    return rows(packed, swapped(packed, -1.0, 1.0))


def chain_kernel(
    slabs, width, faces,
    a0r_ref, a0i_ref, perm_ref, perm_t_ref, ends_ref, d_ref, lead_ref,
    out_ref,
    sk_ref, lhs_ref, w_ref, a_ref, b_ref, m_ref, send_ref, send_back_ref, pa_ref, x_ref, colrow_ref,
    send_sem, recv_sem,
):
    slab = lax.axis_index("slab")
    F = faces
    barrier = pltpu.get_barrier_semaphore()
    for step in (1, slabs - 1):
        pl.semaphore_signal(
            barrier, inc=1, device_id={"slab": lax.rem(slab + step, slabs)}, device_id_type=MESH
        )

    perm = perm_ref[...]
    pieces = split(a0r_ref[...]) + split(a0i_ref[...])
    turned = mmt(rows(*pieces), perm).astype(bf16)
    placed = mm(perm, lanes(*[turned[k * width:(k + 1) * width] for k in range(4)]))
    a_real = placed[:, :width] + placed[:, width:2 * width]
    a_imag = placed[:, 2 * width:3 * width] + placed[:, 3 * width:]
    a_ref[:, :width] = a_real
    a_ref[:, width:] = a_imag
    row = lax.broadcasted_iota(jnp.int32, (width, width), 0)
    col = lax.broadcasted_iota(jnp.int32, (width, width), 1)
    inner = (row < F) & (col < F)
    unit = jnp.where(row == col, 1.0, 0.0)
    modulus = jnp.where(inner, 0.0, jnp.sqrt(a_real * a_real + a_imag * a_imag))
    row_sums = jnp.sum(modulus, axis=1, keepdims=True)
    col_sums = jnp.sum(modulus, axis=0, keepdims=True)
    pa_ref[...] = lanes(a_real[:, :F], a_imag[:, :F])
    open_real = jnp.where(inner, 0.0, a_real)
    open_imag = jnp.where(inner, 0.0, a_imag)
    rh, rl = split(open_real)
    ih, il = split(open_imag)
    left = rows(lanes(rh, rh, rl, ih, ih, il), lanes(ih, ih, il, -rh, -rh, -rl))
    sk_ref[...] = mmt(left, lanes(rh, rl, rh, ih, il, ih))

    @pl.when(slab == 0)
    def _():
        b_ref[...] = lanes(jnp.zeros((F, F), f32), lead_ref[...])

    pl.semaphore_wait(barrier, 2)

    def hand_on(source, target, device, sems):
        return pltpu.make_async_remote_copy(
            src_ref=source, dst_ref=target, send_sem=send_sem.at[sems], recv_sem=recv_sem.at[sems],
            device_id={"slab": device}, device_id_type=MESH,
        )

    forward = hand_on(send_ref, b_ref, lax.rem(slab + 1, slabs), 0)
    backward = hand_on(send_back_ref, m_ref, lax.rem(slab + slabs - 1, slabs), 1)

    @pl.when(slab > 0)
    def _():
        forward.wait_recv()

    face = pa_ref[:F, :] - b_ref[...]
    pa_ref[:F, :] = face
    square = face * face
    face_mod = jnp.sqrt(square[:, :F] + square[:, F:])
    face_rows = jnp.sum(face_mod, axis=1, keepdims=True) + row_sums[:F]
    face_cols = jnp.sum(face_mod, axis=0, keepdims=True) + col_sums[:, :F]
    row_norm = jnp.maximum(jnp.max(row_sums[F:], axis=0, keepdims=True), jnp.max(face_rows, axis=0, keepdims=True))
    col_norm = jnp.maximum(jnp.max(col_sums[:, F:], axis=1, keepdims=True), jnp.max(face_cols, axis=1, keepdims=True))
    scale = 1.0 / (row_norm * col_norm)
    pa = pa_ref[...]
    other = swapped(face, 1.0, -1.0)
    ends = ends_ref[...]
    zero = jnp.zeros((F, F), f32)
    first = rows(face, other, lanes(ends, zero), lanes(zero, -ends))
    over = mmt(left3(first), right3(pa))
    down = mmt(left3(pa), right3(rows(face, -other)))
    inside = lax.broadcasted_iota(jnp.int32, (width, 2 * F), 1) < F
    below = (lax.broadcasted_iota(jnp.int32, (width, 2 * F), 0) >= F) & inside
    for part in range(2):
        base = part * width
        sk_ref[base:base + F, :] += over[part * F:(part + 1) * F]
        column = down if part == 0 else lanes(down[:, F:], down[:, :F])
        sk_ref[base:base + width, :2 * F] += jnp.where(below, column, 0.0)
    sym = unit - scale * sk_ref[:width, :]
    skew = -scale * sk_ref[width:, :]
    lr = scale * over[2 * F:3 * F]
    li = scale * over[3 * F:]

    def thin(real, imag):
        return lanes(left3(rows(real, imag)), left3(rows(-imag, real)))

    for level in range(3):
        w_ref[level, :, :] = rows(right3v(sym), right3v(skew))
        lhs_ref[level, :width, :] = lanes(left3(sym + skew), left3(sym - skew))
        lhs_ref[level, width:, :] = thin(lr, li)
        result = mm(lhs_ref[level], w_ref[level])
        grown = result[:width]
        flipped = grown.T
        sym = 0.5 * (grown + flipped)
        skew = 0.5 * (grown - flipped)
        lr = lr + result[width:width + F]
        li = li + result[width + F:]
    w_ref[3, :, :] = rows(right3v(sym), right3v(skew))
    ur, ui = sym[:F], skew[:F]
    result = mm(
        lanes(left3(rows(lr, li, ur, ui)), left3(rows(-li, lr, -ui, ur))), w_ref[3]
    )
    w1r, w1i = ur + unit[:F], ui
    w2r, w2i = ur + result[2 * F:3 * F], ui + result[3 * F:]
    left = left3(lanes(lr, li, result[:F], result[F:2 * F]))
    right = right3(rows(lanes(w1r, w1i, w2r, w2i), lanes(-w1i, w1r, -w2i, w2r)))
    packed = mmt(left, right)
    both = rows(lanes(ends, zero), lanes(zero, ends))
    packed = mmt(left3(packed), right3(both))

    @pl.when(slab < slabs - 1)
    def _():
        send_ref[...] = packed
        forward.start()

    @pl.when(slab == slabs - 1)
    def _():
        send_back_ref[...] = packed
        backward.start()

    lhs_ref[3, :width, :] = lanes(left3(sym + skew), left3(sym - skew))
    first_g = lhs_ref[0, :width, :]
    part_g = first_g[:, :width].astype(f32) + first_g[:, 2 * width:3 * width].astype(f32) + unit
    part_t = first_g[:, 3 * width:4 * width].astype(f32) + first_g[:, 5 * width:].astype(f32) + unit
    for level in range(1, 4):
        part_g = part_g + mm(lanes(left3(part_g), left3(part_t)), w_ref[level])
        part_t = part_g.T
    grown = mm(lhs_ref[3, :width, :], w_ref[3])
    flipped = grown.T
    last = rows(right3v(0.5 * (grown + flipped)), right3v(0.5 * (grown - flipped)))
    part_g = part_g + mm(lanes(left3(part_g), left3(part_t)), last)
    part_t = part_g.T
    pr = 0.5 * (part_g + part_t)
    pi = 0.5 * (part_g - part_t)
    a_ref[:F, :F] = face[:, :F]
    a_ref[:F, width:width + F] = face[:, F:]
    left = lanes(left3(a_ref[:, :width].T), left3(a_ref[:, width:].T))
    right = rows(right3v(lanes(pr, pi)), right3v(lanes(pi, -pr)))
    block = scale * mm(left, right)
    block_face = lanes(block[:F, :F], block[:F, width:width + F])
    hr, qr = split(block[:, :width])
    hi, qi = split(block[:, width:])
    turned = mm(perm_t_ref[...], lanes(hr, qr, hi, qi))
    back = turned.astype(bf16)
    back = mm(rows(*[back[:, k * width:(k + 1) * width] for k in range(4)]), perm)
    x_ref[0] = back[:width] + back[width:2 * width]
    x_ref[1] = back[2 * width:3 * width] + back[3 * width:]

    @pl.when(slab == slabs - 1)
    def _():
        out_ref[0, 0, :, :, :] = x_ref[...]

    @pl.when(slab < slabs - 1)
    def _():
        column = left3(
            lanes(
                turned[:, :F] + turned[:, width:width + F],
                turned[:, 2 * width:2 * width + F] + turned[:, 3 * width:3 * width + F],
            )
        )
        face_rows = mm(rows(hr[:F], qr[:F], hi[:F], qi[:F]), perm)
        rr = face_rows[:F] + face_rows[F:2 * F]
        ri = face_rows[2 * F:3 * F] + face_rows[3 * F:]
        across = right3v(rows(lanes(rr, ri), lanes(-ri, rr)))
        d = d_ref[...]
        d_both = right3(rows(lanes(d, zero), lanes(zero, d)))
        u = left3(mm(left3(d), right3v(block_face)))
        v = right3v(as_right(mmt(left3(block_face), d_both)))
        k = mmt(u, d_both)
        backward.wait_recv()
        incoming = right3v(as_right(m_ref[...]))

        @pl.when(slab > 0)
        def _():
            send_back_ref[...] = k + mm(left3(mm(u, incoming)), v)
            backward.start()

        more = mm(left3(mm(column, incoming)), across)
        out_ref[0, 0, 0, :, :] = x_ref[0] + more[:, :width]
        out_ref[0, 0, 1, :, :] = x_ref[1] + more[:, width:]

    @pl.when(slab < slabs - 1)
    def _():
        forward.wait_send()

    @pl.when(slab > 0)
    def _():
        backward.wait_send()


def run_chain(a0r, a0i, perm, ends, d_prev, lead):
    width, faces = a0r.shape[-1], ends.shape[0]
    slabs = lax.axis_size("slab")
    vmem = pl.BlockSpec(memory_space=pltpu.VMEM)
    return pl.pallas_call(
        functools.partial(chain_kernel, slabs, width, faces),
        out_shape=jax.ShapeDtypeStruct((1, 1, 2, width, width), f32),
        in_specs=[vmem] * 7,
        out_specs=vmem,
        scratch_shapes=[
            pltpu.VMEM((2 * width, width), f32),
            pltpu.VMEM((4, width + 2 * faces, 6 * width), bf16),
            pltpu.VMEM((4, 6 * width, width), bf16),
            pltpu.VMEM((width, 2 * width), f32),
            pltpu.VMEM((faces, 2 * faces), f32),
            pltpu.VMEM((faces, 2 * faces), f32),
            pltpu.VMEM((faces, 2 * faces), f32),
            pltpu.VMEM((faces, 2 * faces), f32),
            pltpu.VMEM((width, 2 * faces), f32),
            pltpu.VMEM((2, width, width), f32),
            pltpu.VMEM((8, 128), f32),
            pltpu.SemaphoreType.DMA((2,)),
            pltpu.SemaphoreType.DMA((2,)),
        ],
        compiler_params=pltpu.CompilerParams(collective_id=0, has_side_effects=True),
        name="chain",
    )(a0r, a0i, perm, perm.T, ends, d_prev, lead)


def passed_along(value, axis, steps):
    count = lax.axis_size(axis)
    initial, last = (max(0, -steps), min(count, count - steps))
    return lax.ppermute(value, axis, [(source, source + steps) for source in range(initial, last)])


def product(left, right):
    return jnp.matmul(left, right, precision=highest)


def on_device(
    energies, hamiltonian, coupling, green_prev, profile, phonon_weights, source, weight_index, left_face, right_face,
):
    width = hamiltonian.shape[1]
    base = lax.axis_index("energy")
    table_size = phonon_weights.shape[0]
    chosen = jnp.sum(
        phonon_weights[None, :] * (weight_index[0][:, None] == jnp.arange(table_size, dtype=jnp.int32)[None, :]),
        axis=1,
    )
    own = green_prev[0, 0]

    def coef(position):
        return jnp.sum(chosen * (source[0] == position))

    summed = coef(base) * own
    for offset in range(1, SPAN + 1):
        summed = summed + coef(base + offset) * passed_along(own, "energy", -offset)
        summed = summed + coef(base - offset) * passed_along(own, "energy", offset)
    sigma = summed * profile
    unit = jnp.eye(width, dtype=f32)
    a_real = energies[0] * unit - hamiltonian[0] - sigma[0]
    a_imag = BROAD * unit - sigma[1]
    return chain_part(a_real, a_imag, coupling, left_face, right_face)


def chain_part(a_real, a_imag, coupling, left_face, right_face):
    width = a_real.shape[0]
    coup = coupling[0]
    orbitals = jnp.arange(width, dtype=jnp.int32)
    left, right = left_face[0], right_face[0]
    faces = left.shape[0]
    slab, slabs = lax.axis_index("slab"), lax.axis_size("slab")
    hot = left[:, None] == orbitals[None, :]
    on_face = jnp.any(hot, axis=0)
    place = jnp.sum(jnp.where(hot, jnp.arange(faces, dtype=jnp.int32)[:, None], 0), axis=0)
    before = jnp.sum(((orbitals[:, None] < orbitals[None, :]) & ~on_face[:, None]).astype(jnp.int32), axis=0)
    position = jnp.where(on_face, place, faces + before)
    perm = (orbitals[:, None] == position[None, :]).astype(bf16)
    order = (left[:, None] == right[None, :]).astype(f32)
    d_here = product(order, passed_along(coup, "slab", -1))
    d_prev = passed_along(d_here, "slab", 1)
    ends = jnp.where(slab < slabs - 1, d_here.T, d_prev)
    lead = -0.5 * product(coup.T, coup)
    return run_chain(a_real, a_imag, perm, ends, d_prev, lead)


def solution(mesh):
    in_specs = (
        P("energy"),
        P("slab", None, None),
        P("slab", None, None),
        P("energy", "slab", None, None, None),
        P(),
        P(),
        P("energy", None),
        P("energy", None),
        P("slab", None),
        P("slab", None),
    )
    out_specs = P("energy", "slab", None, None, None)
    return jax.shard_map(on_device, mesh=mesh, in_specs=in_specs, out_specs=out_specs, check_vma=False)
```

time: 482 us -> 191 us (0.40)
  the two profiles are of different devices: /device:TPU:6 before, /device:TPU:198 now
where the time goes in v1:
time: 191 us
  Pallas kernels  85.2 us (45%)
  starting transfers between devices  45.9 us (24%)
  waiting for transfers between devices  39 us (20%)
  other arithmetic  15.2 us (8%)
  matrix products  2.55 us (1%)
  local copies, waits for them, and re-layouts  1.95 us (1%)
    pallas_call x1, Pallas kernels, run_chain(): pl.pallas_call(functools.partial(chain_kernel, slabs, width, faces), out_...  85.2 us
    ppermute x12, starting transfers between devices, passed_along(): lax.ppermute(value, axis, [(source, source + steps) for source in range(i...  45.9 us
    ppermute x12, waiting for transfers between devices, passed_along(): lax.ppermute(value, axis, [(source, source + steps) for source in range(i...  39 us
    mul x1, other arithmetic, on_device(): sigma = summed * profile  9.1 us
  transfers between devices with their start and end apart: 12, of which 5 were waited for; matrix products, arithmetic and copies ran while one was open for 4% of the time, Pallas kernels for 0%

profile of v1, /device:TPU:198, one launch (start us, length us, event | category | flops | bytes accessed | tf_op | source)
XLA Modules:
  0.0 190.6 jit_solution(2161559465789445686)
XLA Ops:
  0.0 0.0 copy-start
  0.0 2.3 %collective-permute-start = (f32[2,256,256]{2,1,0:T(8,128)}, f32[2,256,256]{2,1,0:T(8,128)S(1)}, u32[]{:S(2)}, u32[]{:S(2)}) collective-permute-start(f32[2,256,256]{2,1,0:T(8,128)} %bitcast.69), channel_id=1, source_target_pairs={{8,0},{16,8},{24,16},{32,24},{40,32},{48,40},{56,48},{64,56},{72,6... | collective-permute-start | bytes 1572872 | tf_op jit(solution)/shard_map/ppermute | solution.py:288
  2.3 2.2 %collective-permute-start.1 = (f32[2,256,256]{2,1,0:T(8,128)}, f32[2,256,256]{2,1,0:T(8,128)S(1)}, u32[]{:S(2)}, u32[]{:S(2)}) collective-permute-start(f32[2,256,256]{2,1,0:T(8,128)} %bitcast.70), channel_id=1, source_target_pairs={{0,8},{8,16},{16,24},{24,32},{32,40},{40,48},{48,56},{56,64},{64,7... | collective-permute-start | bytes 1572872 | tf_op jit(solution)/shard_map/ppermute | solution.py:288
  4.5 2.7 %collective-permute-start.2 = (f32[2,256,256]{2,1,0:T(8,128)}, f32[2,256,256]{2,1,0:T(8,128)S(1)}, u32[]{:S(2)}, u32[]{:S(2)}) collective-permute-start(f32[2,256,256]{2,1,0:T(8,128)} %bitcast.71), channel_id=1, source_target_pairs={{16,0},{24,8},{32,16},{40,24},{48,32},{56,40},{64,48},{72,56},{80,... | collective-permute-start | bytes 1572872 | tf_op jit(solution)/shard_map/ppermute | solution.py:288
  7.2 6.4 %collective-permute-start.3 = (f32[2,256,256]{2,1,0:T(8,128)}, f32[2,256,256]{2,1,0:T(8,128)S(1)}, u32[]{:S(2)}, u32[]{:S(2)}) collective-permute-start(f32[2,256,256]{2,1,0:T(8,128)} %bitcast.72), channel_id=1, source_target_pairs={{0,16},{8,24},{16,32},{24,40},{32,48},{40,56},{48,64},{56,72},{64,... | collective-permute-start | bytes 1572872 | tf_op jit(solution)/shard_map/ppermute | solution.py:288
  13.7 1.3 collective-permute-start.10
  15.0 0.7 fusion.5
  15.7 0.1 convert_reduce_fusion
  15.8 3.8 %collective-permute-done.10 = f32[64,64]{1,0:T(8,128)S(1)} collective-permute-done((f32[64,64]{1,0:T(8,128)}, f32[64,64]{1,0:T(8,128)S(1)}, u32[]{:S(2)}, u32[]{:S(2)}) %collective-permute-start.10) | collective-permute-done | bytes 16416 | tf_op jit(solution)/shard_map/ppermute | solution.py:288
  19.7 0.9 fusion.6
  20.6 3.5 %collective-permute-start.11 = (f32[64,64]{1,0:T(8,128)S(1)}, f32[64,64]{1,0:T(8,128)S(1)}, u32[]{:S(2)}, u32[]{:S(2)}) collective-permute-start(f32[64,64]{1,0:T(8,128)S(1)} %fusion.6), channel_id=1, source_target_pairs={{0,1},{1,2},{2,3},{3,4},{4,5},{5,6},{6,7},{8,9},{9,10},{10,11},{11... | collective-permute-start | bytes 49160 | tf_op jit(solution)/shard_map/ppermute | solution.py:288
  24.0 0.7 select_reduce_fusion
  25.4 0.2 collective-permute-done.11.d_ref
  25.6 0.0 copy-start.2
  25.6 1.9 %collective-permute-start.4 = (f32[2,256,256]{2,1,0:T(8,128)}, f32[2,256,256]{2,1,0:T(8,128)S(1)}, u32[]{:S(2)}, u32[]{:S(2)}) collective-permute-start(f32[2,256,256]{2,1,0:T(8,128)} %bitcast.73), channel_id=1, source_target_pairs={{24,0},{32,8},{40,16},{48,24},{56,32},{64,40},{72,48},{80,56},{88,... | collective-permute-start | bytes 1572872 | tf_op jit(solution)/shard_map/ppermute | solution.py:288
  27.5 0.9 fusion.10
  28.4 1.7 convolution_multiply_fusion.lead_ref
  30.1 0.0 collective-permute-done
  30.1 7.0 %collective-permute-start.5 = (f32[2,256,256]{2,1,0:T(8,128)}, f32[2,256,256]{2,1,0:T(8,128)}, u32[]{:S(2)}, u32[]{:S(2)}) collective-permute-start(f32[2,256,256]{2,1,0:T(8,128)} %bitcast.74), channel_id=1, source_target_pairs={{0,24},{8,32},{16,40},{24,48},{32,56},{40,64},{48,72},{56,80},{64,... | collective-permute-start | bytes 1572872 | tf_op jit(solution)/shard_map/ppermute | solution.py:288
  37.0 0.0 collective-permute-done.1
  37.1 1.9 %collective-permute-start.6 = (f32[2,256,256]{2,1,0:T(8,128)}, f32[2,256,256]{2,1,0:T(8,128)}, u32[]{:S(2)}, u32[]{:S(2)}) collective-permute-start(f32[2,256,256]{2,1,0:T(8,128)} %bitcast.75), channel_id=1, source_target_pairs={{32,0},{40,8},{48,16},{56,24},{64,32},{72,40},{80,48},{88,56},{96,... | collective-permute-start | bytes 1572872 | tf_op jit(solution)/shard_map/ppermute | solution.py:288
  39.0 0.0 collective-permute-done.2
  39.0 7.5 %collective-permute-start.7 = (f32[2,256,256]{2,1,0:T(8,128)}, f32[2,256,256]{2,1,0:T(8,128)}, u32[]{:S(2)}, u32[]{:S(2)}) collective-permute-start(f32[2,256,256]{2,1,0:T(8,128)} %bitcast.76), channel_id=1, source_target_pairs={{0,32},{8,40},{16,48},{24,56},{32,64},{40,72},{48,80},{56,88},{64,... | collective-permute-start | bytes 1572872 | tf_op jit(solution)/shard_map/ppermute | solution.py:288
  46.5 0.0 collective-permute-done.3
  46.6 1.9 %collective-permute-start.8 = (f32[2,256,256]{2,1,0:T(8,128)}, f32[2,256,256]{2,1,0:T(8,128)}, u32[]{:S(2)}, u32[]{:S(2)}) collective-permute-start(f32[2,256,256]{2,1,0:T(8,128)} %bitcast.77), channel_id=1, source_target_pairs={{40,0},{48,8},{56,16},{64,24},{72,32},{80,40},{88,48},{96,56},{104... | collective-permute-start | bytes 1572872 | tf_op jit(solution)/shard_map/ppermute | solution.py:288
  48.5 0.0 collective-permute-done.4
  48.5 7.3 %collective-permute-start.9 = (f32[2,256,256]{2,1,0:T(8,128)}, f32[2,256,256]{2,1,0:T(8,128)}, u32[]{:S(2)}, u32[]{:S(2)}) collective-permute-start(f32[2,256,256]{2,1,0:T(8,128)} %bitcast.78), channel_id=1, source_target_pairs={{0,40},{8,48},{16,56},{24,64},{32,72},{40,80},{48,88},{56,96},{64,... | collective-permute-start | bytes 1572872 | tf_op jit(solution)/shard_map/ppermute | solution.py:288
  55.8 1.4 fusion.11
  57.1 0.7 fusion.4
  57.9 0.1 copy.12
  58.0 0.0 copy-done.2
  58.0 0.6 bitcast_select_fusion.ends_ref
  58.6 21.3 %collective-permute-done.5 = f32[2,256,256]{2,1,0:T(8,128)} collective-permute-done((f32[2,256,256]{2,1,0:T(8,128)}, f32[2,256,256]{2,1,0:T(8,128)}, u32[]{:S(2)}, u32[]{:S(2)}) %collective-permute-start.5) | collective-permute-done | bytes 524320 | tf_op jit(solution)/shard_map/ppermute | solution.py:288
  79.9 3.4 %collective-permute-done.6 = f32[2,256,256]{2,1,0:T(8,128)} collective-permute-done((f32[2,256,256]{2,1,0:T(8,128)}, f32[2,256,256]{2,1,0:T(8,128)}, u32[]{:S(2)}, u32[]{:S(2)}) %collective-permute-start.6) | collective-permute-done | bytes 524320 | tf_op jit(solution)/shard_map/ppermute | solution.py:288
  83.3 0.0 collective-permute-done.7
  83.3 0.0 collective-permute-done.8
  83.3 10.3 %collective-permute-done.9 = f32[2,256,256]{2,1,0:T(8,128)} collective-permute-done((f32[2,256,256]{2,1,0:T(8,128)}, f32[2,256,256]{2,1,0:T(8,128)}, u32[]{:S(2)}, u32[]{:S(2)}) %collective-permute-start.9) | collective-permute-done | bytes 524320 | tf_op jit(solution)/shard_map/ppermute | solution.py:288
  93.6 0.0 copy-done
  93.6 0.0 copy-start.1
  93.6 9.1 %add_multiply_fusion = f32[2,256,256]{2,1,0:T(8,128)S(1)} fusion(f32[2,256,256]{2,1,0:T(8,128)} %collective-permute-done.9, f32[2,256,256]{2,1,0:T(8,128)} %collective-permute-done.8, f32[2,256,256]{2,1,0:T(8,128)} %collective-permute-done.7, f32[2,256,256]{2,1,0:T(8,128)} %collective-permute-done.6, f32[2,256,256]{2,1,0:T(8,128)} %collective-permute-done.5, ...), kind=kLoop, calls=%fused_computation.1 | loop fusion | flops 2883584 | bytes 6553644 | tf_op jit(solution)/shard_map/mul | solution.py:314
  102.7 0.0 copy-done.1
  102.7 0.8 fusion
  103.5 85.2 %chain.1 = f32[1,1,2,256,256]{4,3,2,1,0:T(8,128)} custom-call(f32[256,256]{1,0:T(8,128)} %get-tuple-element.17.a0r_ref, f32[256,256]{1,0:T(8,128)} %get-tuple-element.16.a0i_ref, bf16[256,256]{1,0:T(8,128)(2,1)} %get-tuple-element.19.perm_ref, bf16[256,256]{1,0:T(8,128)(2,1)} %get-tuple-element.18.perm_t_ref, f32[64,64]{1,0:T(8,128)} %bitcast_select_fusion.ends_ref, ...), custom_call_target="tpu_custom_call" | custom-call | tf_op jit(solution)/shard_map/chain/pallas_call | solution.py:260
  188.7 1.9 copy.15
  (2 shorter events, 0.0 us)
Async XLA Ops:
  0.0 93.6 %copy-start = (f32[1,1,2,256,256]{4,3,2,1,0:T(8,128)S(1)}, f32[1,1,2,256,256]{4,3,2,1,0:T(8,128)}, u32[]{:S(2)}) copy-start(f32[1,1,2,256,256]{4,3,2,1,0:T(8,128)} %param.13) | copy-start | bytes 1572868
  0.0 30.1 %collective-permute-start = (f32[2,256,256]{2,1,0:T(8,128)}, f32[2,256,256]{2,1,0:T(8,128)S(1)}, u32[]{:S(2)}, u32[]{:S(2)}) collective-permute-start(f32[2,256,256]{2,1,0:T(8,128)} %bitcast.69), channel_id=1, source_target_pairs={{8,0},{16,8},{24,16},{32,24},{40,32},{48,40},{56,48},{64,56},{72,6... | collective-permute-start | bytes 1572872 | tf_op jit(solution)/shard_map/ppermute | solution.py:288
  2.3 34.7 %collective-permute-start.1 = (f32[2,256,256]{2,1,0:T(8,128)}, f32[2,256,256]{2,1,0:T(8,128)S(1)}, u32[]{:S(2)}, u32[]{:S(2)}) collective-permute-start(f32[2,256,256]{2,1,0:T(8,128)} %bitcast.70), channel_id=1, source_target_pairs={{0,8},{8,16},{16,24},{24,32},{32,40},{40,48},{48,56},{56,64},{64,7... | collective-permute-start | bytes 1572872 | tf_op jit(solution)/shard_map/ppermute | solution.py:288
  4.5 34.5 %collective-permute-start.2 = (f32[2,256,256]{2,1,0:T(8,128)}, f32[2,256,256]{2,1,0:T(8,128)S(1)}, u32[]{:S(2)}, u32[]{:S(2)}) collective-permute-start(f32[2,256,256]{2,1,0:T(8,128)} %bitcast.71), channel_id=1, source_target_pairs={{16,0},{24,8},{32,16},{40,24},{48,32},{56,40},{64,48},{72,56},{80,... | collective-permute-start | bytes 1572872 | tf_op jit(solution)/shard_map/ppermute | solution.py:288
  7.2 39.3 %collective-permute-start.3 = (f32[2,256,256]{2,1,0:T(8,128)}, f32[2,256,256]{2,1,0:T(8,128)S(1)}, u32[]{:S(2)}, u32[]{:S(2)}) collective-permute-start(f32[2,256,256]{2,1,0:T(8,128)} %bitcast.72), channel_id=1, source_target_pairs={{0,16},{8,24},{16,32},{24,40},{32,48},{40,56},{48,64},{56,72},{64,... | collective-permute-start | bytes 1572872 | tf_op jit(solution)/shard_map/ppermute | solution.py:288
  13.7 6.0 %collective-permute-start.10 = (f32[64,64]{1,0:T(8,128)}, f32[64,64]{1,0:T(8,128)S(1)}, u32[]{:S(2)}, u32[]{:S(2)}) collective-permute-start(f32[64,64]{1,0:T(8,128)} %bitcast.79), channel_id=1, source_target_pairs={{1,0},{2,1},{3,2},{4,3},{5,4},{6,5},{7,6},{9,8},{10,9},{11,10},{12... | collective-permute-start | bytes 49160 | tf_op jit(solution)/shard_map/ppermute | solution.py:288
  20.6 5.1 %collective-permute-start.11 = (f32[64,64]{1,0:T(8,128)S(1)}, f32[64,64]{1,0:T(8,128)S(1)}, u32[]{:S(2)}, u32[]{:S(2)}) collective-permute-start(f32[64,64]{1,0:T(8,128)S(1)} %fusion.6), channel_id=1, source_target_pairs={{0,1},{1,2},{2,3},{3,4},{4,5},{5,6},{6,7},{8,9},{9,10},{10,11},{11... | collective-permute-start | bytes 49160 | tf_op jit(solution)/shard_map/ppermute | solution.py:288
  25.6 32.3 %copy-start.2 = (f32[64,64]{1,0:T(8,128)}, f32[64,64]{1,0:T(8,128)S(1)}, u32[]{:S(2)}) copy-start(f32[64,64]{1,0:T(8,128)S(1)} %collective-permute-done.11.d_ref) | copy-start | bytes 49156
  25.6 22.9 %collective-permute-start.4 = (f32[2,256,256]{2,1,0:T(8,128)}, f32[2,256,256]{2,1,0:T(8,128)S(1)}, u32[]{:S(2)}, u32[]{:S(2)}) collective-permute-start(f32[2,256,256]{2,1,0:T(8,128)} %bitcast.73), channel_id=1, source_target_pairs={{24,0},{32,8},{40,16},{48,24},{56,32},{64,40},{72,48},{80,56},{88,... | collective-permute-start | bytes 1572872 | tf_op jit(solution)/shard_map/ppermute | solution.py:288
  30.1 49.8 %collective-permute-start.5 = (f32[2,256,256]{2,1,0:T(8,128)}, f32[2,256,256]{2,1,0:T(8,128)}, u32[]{:S(2)}, u32[]{:S(2)}) collective-permute-start(f32[2,256,256]{2,1,0:T(8,128)} %bitcast.74), channel_id=1, source_target_pairs={{0,24},{8,32},{16,40},{24,48},{32,56},{40,64},{48,72},{56,80},{64,... | collective-permute-start | bytes 1572872 | tf_op jit(solution)/shard_map/ppermute | solution.py:288
  37.1 46.2 %collective-permute-start.6 = (f32[2,256,256]{2,1,0:T(8,128)}, f32[2,256,256]{2,1,0:T(8,128)}, u32[]{:S(2)}, u32[]{:S(2)}) collective-permute-start(f32[2,256,256]{2,1,0:T(8,128)} %bitcast.75), channel_id=1, source_target_pairs={{32,0},{40,8},{48,16},{56,24},{64,32},{72,40},{80,48},{88,56},{96,... | collective-permute-start | bytes 1572872 | tf_op jit(solution)/shard_map/ppermute | solution.py:288
  39.0 44.3 %collective-permute-start.7 = (f32[2,256,256]{2,1,0:T(8,128)}, f32[2,256,256]{2,1,0:T(8,128)}, u32[]{:S(2)}, u32[]{:S(2)}) collective-permute-start(f32[2,256,256]{2,1,0:T(8,128)} %bitcast.76), channel_id=1, source_target_pairs={{0,32},{8,40},{16,48},{24,56},{32,64},{40,72},{48,80},{56,88},{64,... | collective-permute-start | bytes 1572872 | tf_op jit(solution)/shard_map/ppermute | solution.py:288
  46.6 36.7 %collective-permute-start.8 = (f32[2,256,256]{2,1,0:T(8,128)}, f32[2,256,256]{2,1,0:T(8,128)}, u32[]{:S(2)}, u32[]{:S(2)}) collective-permute-start(f32[2,256,256]{2,1,0:T(8,128)} %bitcast.77), channel_id=1, source_target_pairs={{40,0},{48,8},{56,16},{64,24},{72,32},{80,40},{88,48},{96,56},{104... | collective-permute-start | bytes 1572872 | tf_op jit(solution)/shard_map/ppermute | solution.py:288
  48.5 45.1 %collective-permute-start.9 = (f32[2,256,256]{2,1,0:T(8,128)}, f32[2,256,256]{2,1,0:T(8,128)}, u32[]{:S(2)}, u32[]{:S(2)}) collective-permute-start(f32[2,256,256]{2,1,0:T(8,128)} %bitcast.78), channel_id=1, source_target_pairs={{0,40},{8,48},{16,56},{24,64},{32,72},{40,80},{48,88},{56,96},{64,... | collective-permute-start | bytes 1572872 | tf_op jit(solution)/shard_map/ppermute | solution.py:288
  93.6 9.1 %copy-start.1 = (f32[1,256,256]{2,1,0:T(8,128)S(1)}, f32[1,256,256]{2,1,0:T(8,128)}, u32[]{:S(2)}) copy-start(f32[1,256,256]{2,1,0:T(8,128)} %param.11) | copy-start | bytes 786436

commit v2 on v1

--- a/solution.py
+++ b/solution.py
@@ -6,12 +6,10 @@
 from jax.experimental.pallas import tpu as pltpu
 from jax.sharding import PartitionSpec as P
 
-SPAN = 5
 BROAD = 0.02
 f32 = jnp.float32
 bf16 = jnp.bfloat16
 MESH = pl.DeviceIdType.MESH
-highest = lax.Precision.HIGHEST
 
 
 def mm(left, right):
@@ -61,33 +59,323 @@
     return rows(packed, swapped(packed, -1.0, 1.0))
 
 
-def chain_kernel(
-    slabs, width, faces,
-    a0r_ref, a0i_ref, perm_ref, perm_t_ref, ends_ref, d_ref, lead_ref,
+NX = 4
+CORES = 2
+CHUNKS = 16
+AHEAD = 4
+FAR_LAG = 2
+PARTNER_LAG = 4
+LINE_LAG = 6
+TABLE = 32
+
+
+def where_on_energy():
+    spot = lax.axis_index("energy")
+    core = lax.rem(spot, CORES)
+    chip = lax.div(spot, CORES)
+    return lax.rem(chip, NX), lax.div(chip, NX), core
+
+
+def energy_of(x, z, core):
+    return (z * NX + x) * CORES + core
+
+
+def remote(source, target, send, recv, **device):
+    return pltpu.make_async_remote_copy(
+        src_ref=source, dst_ref=target, send_sem=send, recv_sem=recv, device_id=device, device_id_type=MESH
+    )
+
+
+def greet(lines, slabs):
+    x, z, core = where_on_energy()
+    barrier = pltpu.get_barrier_semaphore()
+
+    def signal(**device):
+        pl.semaphore_signal(barrier, inc=1, device_id=device, device_id_type=MESH)
+
+    signal(energy=energy_of(lax.rem(x + 1, NX), z, core))
+    signal(energy=energy_of(lax.rem(x + NX - 1, NX), z, core))
+    signal(energy=energy_of(x, z, 1 - core))
+    count = 3
+    for step, there in ((1, z < lines - 1), (-1, z > 0)):
+        @pl.when(there)
+        def _():
+            signal(energy=energy_of(x, z + step, core))
+            signal(energy=energy_of(x, z + step, 1 - core))
+        count = count + 2 * there.astype(jnp.int32)
+    if slabs > 1:
+        slab = lax.axis_index("slab")
+        for step in (1, slabs - 1):
+            signal(slab=lax.rem(slab + step, slabs))
+        count = count + 2
+    return barrier, count
+
+
+def make_table(source_ref, index_ref, weights_ref, table_ref):
+    here = lax.axis_index("energy")
+    row = lax.broadcasted_iota(jnp.int32, (TABLE, 128), 0)
+    total = jnp.zeros((TABLE, 128), f32)
+    for term in range(2):
+        weight = weights_ref[index_ref[0, term]]
+        distance = source_ref[0, term] - here + TABLE // 2
+        total = total + jnp.where(row == distance, weight, 0.0)
+    table_ref[0] = total
+
+
+def exchange(lines, own, table_ref, got, part_send, part_recv, line_send, line_recv, acc,
+             send_sem, recv_sem, table_send, table_recv, meanwhile, finish):
+    x, z, core = where_on_energy()
+    depth = own.shape[0] // CHUNKS
+    right = energy_of(lax.rem(x + 1, NX), z, core)
+    left = energy_of(lax.rem(x + NX - 1, NX), z, core)
+    partner = energy_of(x, z, 1 - core)
+    up_there, down_there = z < lines - 1, z > 0
+    up, down = energy_of(x, z + 1, core), energy_of(x, z - 1, core)
+    up_other, down_other = energy_of(x, z + 1, 1 - core), energy_of(x, z - 1, 1 - core)
+
+    def part(ref, chunk):
+        return ref.at[pl.ds(chunk * depth, depth), :]
+
+    def tables(flow, device):
+        return remote(table_ref.at[0], table_ref.at[flow + 1], table_send.at[flow], table_recv.at[flow], energy=device)
+
+    to_partner = tables(0, partner)
+    to_up, to_up_other = tables(3, up), tables(4, up_other)
+    to_down, to_down_other = tables(1, down), tables(2, down_other)
+
+    def piece(flow, chunk, source, target, device):
+        return remote(source, target, send_sem.at[flow, chunk], recv_sem.at[flow, chunk], energy=device)
+
+    to_right = [piece(0, q, part(own, q), part(got.at[0], q), right) for q in range(CHUNKS)]
+    to_left = [piece(1, q, part(own, q), part(got.at[1], q), left) for q in range(CHUNKS)]
+    onward = [
+        piece(2, q, part(got.at[q % 2], q), part(got.at[2], q), right if q % 2 == 0 else left)
+        for q in range(CHUNKS)
+    ]
+    across = [
+        [piece(3 + k, q, part(part_send.at[k], q), part(part_recv.at[k], q), partner) for q in range(CHUNKS)]
+        for k in range(3)
+    ]
+    upward = [piece(6, q, part(line_send.at[0], q), part(line_recv.at[0], q), up) for q in range(CHUNKS)]
+    downward = [piece(7, q, part(line_send.at[1], q), part(line_recv.at[1], q), down) for q in range(CHUNKS)]
+
+    def own_start(chunk):
+        to_right[chunk].start()
+        to_left[chunk].start()
+
+    for chunk in range(AHEAD):
+        own_start(chunk)
+    to_partner.start()
+
+    @pl.when(up_there)
+    def _():
+        to_up.start()
+        to_up_other.start()
+
+    @pl.when(down_there)
+    def _():
+        to_down.start()
+        to_down_other.start()
+
+    meanwhile()
+    to_partner.wait()
+
+    @pl.when(up_there)
+    def _():
+        to_up.wait_send()
+        to_up_other.wait_send()
+        to_down.wait_recv()
+        to_down_other.wait_recv()
+
+    @pl.when(down_there)
+    def _():
+        to_down.wait_send()
+        to_down_other.wait_send()
+        to_up.wait_recv()
+        to_up_other.wait_recv()
+
+    apart = [0] + [lax.rem(x + step, NX) - x for step in (3, 1, 2)]
+
+    def weighted(slot, line, other, chunk):
+        total = None
+        for k in range(4):
+            lag = 2 * apart[k] + (2 * core - 1 if other else 0) - 8 * line + TABLE // 2
+            weight = table_ref[slot, pl.ds(lag, 1), :]
+            block = (own if k == 0 else got.at[k - 1])[pl.ds(chunk * depth, depth), :]
+            term = lanes(weight, weight) * block
+            total = term if total is None else total + term
+        return total
+
+    for step in range(CHUNKS + LINE_LAG):
+        q = step
+        if q < CHUNKS:
+            to_right[q].wait_recv()
+            to_left[q].wait_recv()
+            onward[q].start()
+            if q + AHEAD < CHUNKS:
+                own_start(q + AHEAD)
+        q = step - FAR_LAG
+        if 0 <= q < CHUNKS:
+            onward[q].wait_recv()
+            piece_rows = pl.ds(q * depth, depth)
+            acc[piece_rows, :] = weighted(0, 0, False, q)
+            part_send[0, piece_rows, :] = weighted(1, 0, True, q)
+            across[0][q].start()
+
+            @pl.when(up_there)
+            def _():
+                line_send[0, piece_rows, :] = weighted(2, 1, False, q)
+                part_send[1, piece_rows, :] = weighted(3, 1, True, q)
+                across[1][q].start()
+
+            @pl.when(down_there)
+            def _():
+                line_send[1, piece_rows, :] = weighted(4, -1, False, q)
+                part_send[2, piece_rows, :] = weighted(5, -1, True, q)
+                across[2][q].start()
+        q = step - PARTNER_LAG
+        if 0 <= q < CHUNKS:
+            piece_rows = pl.ds(q * depth, depth)
+            across[0][q].wait_recv()
+            acc[piece_rows, :] += part_recv[0, piece_rows, :]
+
+            @pl.when(up_there)
+            def _():
+                across[1][q].wait_recv()
+                line_send[0, piece_rows, :] += part_recv[1, piece_rows, :]
+                upward[q].start()
+
+            @pl.when(down_there)
+            def _():
+                across[2][q].wait_recv()
+                line_send[1, piece_rows, :] += part_recv[2, piece_rows, :]
+                downward[q].start()
+        q = step - LINE_LAG
+        if 0 <= q < CHUNKS:
+            piece_rows = pl.ds(q * depth, depth)
+
+            @pl.when(down_there)
+            def _():
+                upward[q].wait_recv()
+                acc[piece_rows, :] += line_recv[0, piece_rows, :]
+
+            @pl.when(up_there)
+            def _():
+                downward[q].wait_recv()
+                acc[piece_rows, :] += line_recv[1, piece_rows, :]
+
+            finish(q, depth)
+
+    def settle():
+        for q in range(CHUNKS):
+            to_right[q].wait_send()
+            to_left[q].wait_send()
+            onward[q].wait_send()
+            across[0][q].wait_send()
+
+            @pl.when(up_there)
+            def _():
+                across[1][q].wait_send()
+                upward[q].wait_send()
+
+            @pl.when(down_there)
+            def _():
+                across[2][q].wait_send()
+                downward[q].wait_send()
+
+    return settle
+
+
+EXCHANGE_SCRATCH = lambda width: [
+    pltpu.VMEM((6, TABLE, 128), f32),
+    pltpu.VMEM((3, 2 * width, width), f32),
+    pltpu.VMEM((3, 2 * width, width), f32),
+    pltpu.VMEM((3, 2 * width, width), f32),
+    pltpu.VMEM((2, 2 * width, width), f32),
+    pltpu.VMEM((2, 2 * width, width), f32),
+    pltpu.VMEM((2 * width, width), f32),
+    pltpu.SemaphoreType.DMA((8, CHUNKS)),
+    pltpu.SemaphoreType.DMA((8, CHUNKS)),
+    pltpu.SemaphoreType.DMA((5,)),
+    pltpu.SemaphoreType.DMA((5,)),
+]
+
+
+def born_kernel(
+    lines, slabs, width, faces,
+    energy_ref, source_ref, index_ref, weights_ref, green_ref, ham_ref, profile_ref, coup_ref, left_ref, right_ref,
     out_ref,
-    sk_ref, lhs_ref, w_ref, a_ref, b_ref, m_ref, send_ref, send_back_ref, pa_ref, x_ref, colrow_ref,
+    table_ref, got, part_send, part_recv, line_send, line_recv, acc, piece_send, piece_recv, table_send, table_recv,
+    perm_ref, perm_t_ref, next_ref, d_here_ref, d_ref, ends_ref, lead_ref,
+    sk_ref, lhs_ref, w_ref, a_ref, b_ref, m_ref, send_ref, send_back_ref, pa_ref, x_ref,
     send_sem, recv_sem,
 ):
     slab = lax.axis_index("slab")
     F = faces
-    barrier = pltpu.get_barrier_semaphore()
-    for step in (1, slabs - 1):
-        pl.semaphore_signal(
-            barrier, inc=1, device_id={"slab": lax.rem(slab + step, slabs)}, device_id_type=MESH
+    row = lax.broadcasted_iota(jnp.int32, (width, width), 0)
+    col = lax.broadcasted_iota(jnp.int32, (width, width), 1)
+    unit = jnp.where(row == col, 1.0, 0.0)
+    barrier, greetings = greet(lines, slabs)
+    make_table(source_ref, index_ref, weights_ref, table_ref)
+    pl.semaphore_wait(barrier, greetings)
+    after, ahead_of = lax.rem(slab + 1, slabs), lax.rem(slab + slabs - 1, slabs)
+    forward = remote(send_ref, b_ref, send_sem.at[0], recv_sem.at[0], slab=after)
+    backward = remote(send_back_ref, m_ref, send_sem.at[1], recv_sem.at[1], slab=ahead_of)
+    give_coupling = remote(coup_ref, next_ref, send_sem.at[2], recv_sem.at[2], slab=ahead_of)
+    give_d = remote(d_here_ref, d_ref, send_sem.at[3], recv_sem.at[3], slab=after)
+    zero = jnp.zeros((F, F), f32)
+
+    def meanwhile():
+        give_coupling.start()
+        spot = lax.broadcasted_iota(jnp.int32, (width, F), 0)
+        hot_left = jnp.where(spot == left_ref[...], 1.0, 0.0)
+        hot_right = jnp.where(spot == right_ref[...], 1.0, 0.0)
+        on_face = jnp.sum(hot_left, axis=1, keepdims=True)
+        off_face = jnp.broadcast_to(1.0 - on_face, (width, 128)).astype(bf16)
+        before = mm(jnp.where(col < row, 1.0, 0.0).astype(bf16), off_face)[:, :1]
+        rest = jnp.where(col == F + before.astype(jnp.int32), 1.0 - on_face, 0.0)
+        perm_t = rest + lanes(hot_left, jnp.zeros((width, width - F), f32))
+        perm_t_ref[...] = perm_t.astype(bf16)
+        perm_ref[...] = perm_t.T.astype(bf16)
+        order = mm(hot_left.T.astype(bf16), hot_right.astype(bf16)).astype(bf16)
+        coup = coup_ref[...]
+        lead_ref[...] = -0.5 * mm(left3(coup.T), right3v(coup))
+        give_coupling.wait()
+        high, low = split(next_ref[...])
+        lowest = (next_ref[...] - high.astype(f32) - low.astype(f32)).astype(bf16)
+        d_here_ref[...] = mm(lanes(order, order, order), rows(high, low, lowest))
+        give_d.start()
+        give_d.wait()
+        ends_ref[...] = jnp.where(slab < slabs - 1, d_here_ref[...].T, d_ref[...])
+
+    def finish(chunk, depth):
+        piece_rows = pl.ds(chunk * depth, depth)
+        first = chunk * depth
+        imag = first >= width
+        there = pl.ds(first - width if imag else first, depth)
+        diagonal = jnp.where(
+            lax.broadcasted_iota(jnp.int32, (depth, width), 0) + (first - width if imag else first)
+            == lax.broadcasted_iota(jnp.int32, (depth, width), 1),
+            1.0, 0.0,
         )
+        sigma = profile_ref[there, :] * acc[piece_rows, :]
+        if imag:
+            acc[piece_rows, :] = BROAD * diagonal - sigma
+        else:
+            acc[piece_rows, :] = energy_ref[...] * diagonal - ham_ref[there, :] - sigma
+
+    settle = exchange(lines, green_ref, table_ref, got, part_send, part_recv, line_send, line_recv, acc,
+                      piece_send, piece_recv, table_send, table_recv, meanwhile, finish)
 
     perm = perm_ref[...]
-    pieces = split(a0r_ref[...]) + split(a0i_ref[...])
+    pieces = split(acc[:width, :]) + split(acc[width:, :])
     turned = mmt(rows(*pieces), perm).astype(bf16)
     placed = mm(perm, lanes(*[turned[k * width:(k + 1) * width] for k in range(4)]))
     a_real = placed[:, :width] + placed[:, width:2 * width]
     a_imag = placed[:, 2 * width:3 * width] + placed[:, 3 * width:]
     a_ref[:, :width] = a_real
     a_ref[:, width:] = a_imag
-    row = lax.broadcasted_iota(jnp.int32, (width, width), 0)
-    col = lax.broadcasted_iota(jnp.int32, (width, width), 1)
     inner = (row < F) & (col < F)
-    unit = jnp.where(row == col, 1.0, 0.0)
     modulus = jnp.where(inner, 0.0, jnp.sqrt(a_real * a_real + a_imag * a_imag))
     row_sums = jnp.sum(modulus, axis=1, keepdims=True)
     col_sums = jnp.sum(modulus, axis=0, keepdims=True)
@@ -102,17 +390,6 @@
     @pl.when(slab == 0)
     def _():
         b_ref[...] = lanes(jnp.zeros((F, F), f32), lead_ref[...])
-
-    pl.semaphore_wait(barrier, 2)
-
-    def hand_on(source, target, device, sems):
-        return pltpu.make_async_remote_copy(
-            src_ref=source, dst_ref=target, send_sem=send_sem.at[sems], recv_sem=recv_sem.at[sems],
-            device_id={"slab": device}, device_id_type=MESH,
-        )
-
-    forward = hand_on(send_ref, b_ref, lax.rem(slab + 1, slabs), 0)
-    backward = hand_on(send_back_ref, m_ref, lax.rem(slab + slabs - 1, slabs), 1)
 
     @pl.when(slab > 0)
     def _():
@@ -130,7 +407,6 @@
     pa = pa_ref[...]
     other = swapped(face, 1.0, -1.0)
     ends = ends_ref[...]
-    zero = jnp.zeros((F, F), f32)
     first = rows(face, other, lanes(ends, zero), lanes(zero, -ends))
     over = mmt(left3(first), right3(pa))
     down = mmt(left3(pa), right3(rows(face, -other)))
@@ -251,92 +527,42 @@
     @pl.when(slab > 0)
     def _():
         backward.wait_send()
-
-
-def run_chain(a0r, a0i, perm, ends, d_prev, lead):
-    width, faces = a0r.shape[-1], ends.shape[0]
-    slabs = lax.axis_size("slab")
-    vmem = pl.BlockSpec(memory_space=pltpu.VMEM)
+    settle()
+
+
+def run(energies, hamiltonian, coupling, green_prev, profile, phonon_weights, source, weight_index, left, right):
+    width, faces = hamiltonian.shape[-1], coupling.shape[-1]
+    slabs, lines = lax.axis_size("slab"), lax.axis_size("energy") // (NX * CORES)
+    vmem, smem = pl.BlockSpec(memory_space=pltpu.VMEM), pl.BlockSpec(memory_space=pltpu.SMEM)
+    face_block = pltpu.VMEM((faces, faces), f32)
+    face_pair = pltpu.VMEM((faces, 2 * faces), f32)
     return pl.pallas_call(
-        functools.partial(chain_kernel, slabs, width, faces),
+        functools.partial(born_kernel, lines, slabs, width, faces),
         out_shape=jax.ShapeDtypeStruct((1, 1, 2, width, width), f32),
-        in_specs=[vmem] * 7,
+        in_specs=[vmem, smem, smem, smem] + [vmem] * 6,
         out_specs=vmem,
-        scratch_shapes=[
+        scratch_shapes=EXCHANGE_SCRATCH(width) + [
+            pltpu.VMEM((width, width), bf16),
+            pltpu.VMEM((width, width), bf16),
+            face_block, face_block, face_block, face_block, face_block,
             pltpu.VMEM((2 * width, width), f32),
             pltpu.VMEM((4, width + 2 * faces, 6 * width), bf16),
             pltpu.VMEM((4, 6 * width, width), bf16),
             pltpu.VMEM((width, 2 * width), f32),
-            pltpu.VMEM((faces, 2 * faces), f32),
-            pltpu.VMEM((faces, 2 * faces), f32),
-            pltpu.VMEM((faces, 2 * faces), f32),
-            pltpu.VMEM((faces, 2 * faces), f32),
+            face_pair, face_pair, face_pair, face_pair,
             pltpu.VMEM((width, 2 * faces), f32),
             pltpu.VMEM((2, width, width), f32),
-            pltpu.VMEM((8, 128), f32),
-            pltpu.SemaphoreType.DMA((2,)),
-            pltpu.SemaphoreType.DMA((2,)),
+            pltpu.SemaphoreType.DMA((4,)),
+            pltpu.SemaphoreType.DMA((4,)),
         ],
-        compiler_params=pltpu.CompilerParams(collective_id=0, has_side_effects=True),
-        name="chain",
-    )(a0r, a0i, perm, perm.T, ends, d_prev, lead)
-
-
-def passed_along(value, axis, steps):
-    count = lax.axis_size(axis)
-    initial, last = (max(0, -steps), min(count, count - steps))
-    return lax.ppermute(value, axis, [(source, source + steps) for source in range(initial, last)])
-
-
-def product(left, right):
-    return jnp.matmul(left, right, precision=highest)
-
-
-def on_device(
-    energies, hamiltonian, coupling, green_prev, profile, phonon_weights, source, weight_index, left_face, right_face,
-):
-    width = hamiltonian.shape[1]
-    base = lax.axis_index("energy")
-    table_size = phonon_weights.shape[0]
-    chosen = jnp.sum(
-        phonon_weights[None, :] * (weight_index[0][:, None] == jnp.arange(table_size, dtype=jnp.int32)[None, :]),
-        axis=1,
+        compiler_params=pltpu.CompilerParams(
+            collective_id=0, has_side_effects=True, vmem_limit_bytes=48 * 1024 * 1024
+        ),
+        name="born",
+    )(
+        energies.reshape(1, 1), source, weight_index, phonon_weights,
+        green_prev.reshape(2 * width, width), hamiltonian[0], profile, coupling[0], left, right,
     )
-    own = green_prev[0, 0]
-
-    def coef(position):
-        return jnp.sum(chosen * (source[0] == position))
-
-    summed = coef(base) * own
-    for offset in range(1, SPAN + 1):
-        summed = summed + coef(base + offset) * passed_along(own, "energy", -offset)
-        summed = summed + coef(base - offset) * passed_along(own, "energy", offset)
-    sigma = summed * profile
-    unit = jnp.eye(width, dtype=f32)
-    a_real = energies[0] * unit - hamiltonian[0] - sigma[0]
-    a_imag = BROAD * unit - sigma[1]
-    return chain_part(a_real, a_imag, coupling, left_face, right_face)
-
-
-def chain_part(a_real, a_imag, coupling, left_face, right_face):
-    width = a_real.shape[0]
-    coup = coupling[0]
-    orbitals = jnp.arange(width, dtype=jnp.int32)
-    left, right = left_face[0], right_face[0]
-    faces = left.shape[0]
-    slab, slabs = lax.axis_index("slab"), lax.axis_size("slab")
-    hot = left[:, None] == orbitals[None, :]
-    on_face = jnp.any(hot, axis=0)
-    place = jnp.sum(jnp.where(hot, jnp.arange(faces, dtype=jnp.int32)[:, None], 0), axis=0)
-    before = jnp.sum(((orbitals[:, None] < orbitals[None, :]) & ~on_face[:, None]).astype(jnp.int32), axis=0)
-    position = jnp.where(on_face, place, faces + before)
-    perm = (orbitals[:, None] == position[None, :]).astype(bf16)
-    order = (left[:, None] == right[None, :]).astype(f32)
-    d_here = product(order, passed_along(coup, "slab", -1))
-    d_prev = passed_along(d_here, "slab", 1)
-    ends = jnp.where(slab < slabs - 1, d_here.T, d_prev)
-    lead = -0.5 * product(coup.T, coup)
-    return run_chain(a_real, a_imag, perm, ends, d_prev, lead)
 
 
 def solution(mesh):
@@ -353,4 +579,4 @@
         P("slab", None),
     )
     out_specs = P("energy", "slab", None, None, None)
-    return jax.shard_map(on_device, mesh=mesh, in_specs=in_specs, out_specs=out_specs, check_vma=False)
+    return jax.shard_map(run, mesh=mesh, in_specs=in_specs, out_specs=out_specs, check_vma=False)

time: 191 us -> 135 us (0.71)
  the two profiles are of different devices: /device:TPU:198 before, /device:TPU:6 now
where the time goes in v2:
time: 135 us
  Pallas kernels  129 us (96%)
  local copies, waits for them, and re-layouts  5.17 us (4%)
    pallas_call x1, Pallas kernels, run(): pl.pallas_call(functools.partial(born_kernel, lines, slabs, width, faces)...  129 us
    unnamed x19, local copies, waits for them, and re-layouts  5.17 us

profile of v2, /device:TPU:6, one launch (start us, length us, event | category | flops | bytes accessed | tf_op | source)
XLA Modules:
  0.0 134.6 jit_solution(488734631669084992)
XLA Ops:
  0.7 0.0 copy-start.7
  0.7 0.0 copy-start.8
  0.7 0.0 copy-start.4
  0.7 0.0 copy-start.5
  0.7 0.0 copy-start.6
  0.7 0.6 copy-done.7
  1.3 0.0 copy-done.8
  1.3 0.0 copy-done.4
  1.3 0.0 copy-done.5
  1.4 0.0 copy-done.6
  1.4 0.0 copy-start
  1.4 1.0 copy-done
  2.4 0.0 copy-start.1
  2.4 0.9 copy-done.1
  3.4 0.0 copy-start.2
  3.4 0.9 copy-done.2
  4.3 0.0 copy-start.3
  4.3 0.8 copy-done.3
  5.1 128.8 %born.1 = f32[1,1,2,256,256]{4,3,2,1,0:T(8,128)S(1)} custom-call(f32[1,1]{1,0:T(1,128)} %bitcast.4.energy_ref, s32[1,2]{1,0:T(1,128)S(1)} %copy-done.4, s32[1,2]{1,0:T(1,128)S(1)} %copy-done.5, f32[8]{0:T(128)S(1)} %copy-done.6, f32[512,256]{1,0:T(8,128)S(1)} %bitcast.5, f32[256,256]{1,0:T(8,128)S(1)} %bitcast.6, f32[256,256]{1,0:T(8,128)S(1)} %copy-done.2, ...), custom_call_target="tpu_custom_call" | custom-call | tf_op jit(solution)/shard_map/born/pallas_call | solution.py:539
  133.9 0.8 copy.13
Async XLA Ops:
  0.7 0.7 copy-start.7
  0.7 0.7 copy-start.8
  0.7 0.7 copy-start.4
  0.7 0.7 copy-start.5
  0.7 0.7 copy-start.6
  1.4 1.0 copy-start
  2.4 0.9 copy-start.1
  3.4 0.9 copy-start.2
  4.3 0.8 copy-start.3

commit v3 on v2

--- a/solution.py
+++ b/solution.py
@@ -55,17 +55,35 @@
     return jnp.where(lane < half, low_sign * turned, high_sign * turned)
 
 
+def put(ref, value):
+    high, low = split(value)
+    ref[0] = high
+    ref[1] = low
+
+
+def tripled(ref):
+    return lanes(ref[0], ref[0], ref[1])
+
+
+def as_weights(sym_ref, skew_ref):
+    return rows(sym_ref[0], sym_ref[1], sym_ref[0], skew_ref[0], skew_ref[1], skew_ref[0])
+
+
+def across_of(real, imag):
+    return right3v(rows(lanes(real, imag), lanes(-imag, real)))
+
+
 def as_right(packed):
     return rows(packed, swapped(packed, -1.0, 1.0))
 
 
 NX = 4
 CORES = 2
-CHUNKS = 16
-AHEAD = 4
+CHUNKS = 8
+AHEAD = 3
 FAR_LAG = 2
-PARTNER_LAG = 4
-LINE_LAG = 6
+PARTNER_LAG = 3
+LINE_LAG = 5
 TABLE = 32
 
 
@@ -105,9 +123,9 @@
         count = count + 2 * there.astype(jnp.int32)
     if slabs > 1:
         slab = lax.axis_index("slab")
-        for step in (1, slabs - 1):
+        for step in range(1, slabs):
             signal(slab=lax.rem(slab + step, slabs))
-        count = count + 2
+        count = count + slabs - 1
     return barrier, count
 
 
@@ -177,7 +195,7 @@
         to_down.start()
         to_down_other.start()
 
-    meanwhile()
+    meanwhile[0]()
     to_partner.wait()
 
     @pl.when(up_there)
@@ -214,6 +232,8 @@
             onward[q].start()
             if q + AHEAD < CHUNKS:
                 own_start(q + AHEAD)
+        if step in (1, 3):
+            meanwhile[(step + 1) // 2]()
         q = step - FAR_LAG
         if 0 <= q < CHUNKS:
             onward[q].wait_recv()
@@ -306,9 +326,9 @@
     energy_ref, source_ref, index_ref, weights_ref, green_ref, ham_ref, profile_ref, coup_ref, left_ref, right_ref,
     out_ref,
     table_ref, got, part_send, part_recv, line_send, line_recv, acc, piece_send, piece_recv, table_send, table_recv,
-    perm_ref, perm_t_ref, next_ref, d_here_ref, d_ref, ends_ref, lead_ref,
-    sk_ref, lhs_ref, w_ref, a_ref, b_ref, m_ref, send_ref, send_back_ref, pa_ref, x_ref,
-    send_sem, recv_sem,
+    perm_ref, perm_t_ref, next_ref, order_ref, d_all, face_all, ends_ref, lead_ref,
+    sk_ref, g_ref, t_ref, s_ref, k_ref, thin_ref, a_ref, b_ref, m_ref, send_ref, part_ref, pa_ref, x_ref,
+    send_sem, recv_sem, spread_sem, d_sem, face_sem,
 ):
     slab = lax.axis_index("slab")
     F = faces
@@ -318,14 +338,27 @@
     barrier, greetings = greet(lines, slabs)
     make_table(source_ref, index_ref, weights_ref, table_ref)
     pl.semaphore_wait(barrier, greetings)
-    after, ahead_of = lax.rem(slab + 1, slabs), lax.rem(slab + slabs - 1, slabs)
-    forward = remote(send_ref, b_ref, send_sem.at[0], recv_sem.at[0], slab=after)
-    backward = remote(send_back_ref, m_ref, send_sem.at[1], recv_sem.at[1], slab=ahead_of)
-    give_coupling = remote(coup_ref, next_ref, send_sem.at[2], recv_sem.at[2], slab=ahead_of)
-    give_d = remote(d_here_ref, d_ref, send_sem.at[3], recv_sem.at[3], slab=after)
+    last = slabs - 1
+    forward = remote(send_ref, b_ref, send_sem.at[0], recv_sem.at[0], slab=lax.rem(slab + 1, slabs))
+    give_coupling = remote(coup_ref, next_ref, send_sem.at[1], recv_sem.at[1], slab=lax.rem(slab + last, slabs))
+    messages = [remote(send_ref, m_ref, spread_sem.at[0, t], recv_sem.at[2], slab=t) for t in range(last)]
+    give_d = [
+        remote(d_all.at[slab], d_all.at[slab], spread_sem.at[1, t], d_sem.at[slab], slab=t) for t in range(slabs)
+    ]
+    give_face = [
+        remote(face_all.at[slab], face_all.at[slab], spread_sem.at[2, t], face_sem.at[slab], slab=t)
+        for t in range(last)
+    ]
+
+    def d_goes(t):
+        return (slab == last - 1) if t == last else ((slab > t) & (slab < last - 1))
+
+    def face_goes(t):
+        return (slab > t) & (slab < last)
+
     zero = jnp.zeros((F, F), f32)
 
-    def meanwhile():
+    def first_stage():
         give_coupling.start()
         spot = lax.broadcasted_iota(jnp.int32, (width, F), 0)
         hot_left = jnp.where(spot == left_ref[...], 1.0, 0.0)
@@ -337,16 +370,35 @@
         perm_t = rest + lanes(hot_left, jnp.zeros((width, width - F), f32))
         perm_t_ref[...] = perm_t.astype(bf16)
         perm_ref[...] = perm_t.T.astype(bf16)
-        order = mm(hot_left.T.astype(bf16), hot_right.astype(bf16)).astype(bf16)
+        order_ref[...] = mm(hot_left.T.astype(bf16), hot_right.astype(bf16)).astype(bf16)
         coup = coup_ref[...]
         lead_ref[...] = -0.5 * mm(left3(coup.T), right3v(coup))
+
+    def second_stage():
         give_coupling.wait()
-        high, low = split(next_ref[...])
-        lowest = (next_ref[...] - high.astype(f32) - low.astype(f32)).astype(bf16)
-        d_here_ref[...] = mm(lanes(order, order, order), rows(high, low, lowest))
-        give_d.start()
-        give_d.wait()
-        ends_ref[...] = jnp.where(slab < slabs - 1, d_here_ref[...].T, d_ref[...])
+        following = next_ref[...]
+        high, low = split(following)
+        lowest = (following - high.astype(f32) - low.astype(f32)).astype(bf16)
+        order = order_ref[...]
+        here = mm(lanes(order, order, order), rows(high, low, lowest))
+        d_all[slab] = here
+        ends_ref[...] = here.T
+        for t in range(slabs):
+            @pl.when(d_goes(t))
+            def _():
+                give_d[t].start()
+
+    def third_stage():
+        def arrived(t, carry):
+            remote(d_all.at[t], d_all.at[t], spread_sem.at[1, 0], d_sem.at[t], slab=slab).wait_recv()
+            return carry
+
+        lax.fori_loop(slab + 1, last - 1, arrived, 0)
+
+        @pl.when(slab == last)
+        def _():
+            arrived(last - 1, 0)
+            ends_ref[...] = d_all[last - 1]
 
     def finish(chunk, depth):
         piece_rows = pl.ds(chunk * depth, depth)
@@ -365,7 +417,8 @@
             acc[piece_rows, :] = energy_ref[...] * diagonal - ham_ref[there, :] - sigma
 
     settle = exchange(lines, green_ref, table_ref, got, part_send, part_recv, line_send, line_recv, acc,
-                      piece_send, piece_recv, table_send, table_recv, meanwhile, finish)
+                      piece_send, piece_recv, table_send, table_recv,
+                      (first_stage, second_stage, third_stage), finish)
 
     perm = perm_ref[...]
     pieces = split(acc[:width, :]) + split(acc[width:, :])
@@ -422,24 +475,26 @@
     lr = scale * over[2 * F:3 * F]
     li = scale * over[3 * F:]
 
-    def thin(real, imag):
-        return lanes(left3(rows(real, imag)), left3(rows(-imag, real)))
-
     for level in range(3):
-        w_ref[level, :, :] = rows(right3v(sym), right3v(skew))
-        lhs_ref[level, :width, :] = lanes(left3(sym + skew), left3(sym - skew))
-        lhs_ref[level, width:, :] = thin(lr, li)
-        result = mm(lhs_ref[level], w_ref[level])
-        grown = result[:width]
+        put(s_ref.at[level], sym)
+        put(k_ref.at[level], skew)
+        put(g_ref.at[level], sym + skew)
+        put(t_ref.at[level], sym - skew)
+        put(thin_ref.at[0], rows(lr, li))
+        put(thin_ref.at[1], rows(-li, lr))
+        weights = as_weights(s_ref.at[level], k_ref.at[level])
+        grown = mm(lanes(tripled(g_ref.at[level]), tripled(t_ref.at[level])), weights)
         flipped = grown.T
         sym = 0.5 * (grown + flipped)
         skew = 0.5 * (grown - flipped)
-        lr = lr + result[width:width + F]
-        li = li + result[width + F:]
-    w_ref[3, :, :] = rows(right3v(sym), right3v(skew))
+        result = mm(lanes(tripled(thin_ref.at[0]), tripled(thin_ref.at[1])), weights)
+        lr = lr + result[:F]
+        li = li + result[F:]
+    put(s_ref.at[3], sym)
+    put(k_ref.at[3], skew)
     ur, ui = sym[:F], skew[:F]
     result = mm(
-        lanes(left3(rows(lr, li, ur, ui)), left3(rows(-li, lr, -ui, ur))), w_ref[3]
+        lanes(left3(rows(lr, li, ur, ui)), left3(rows(-li, lr, -ui, ur))), as_weights(s_ref.at[3], k_ref.at[3])
     )
     w1r, w1i = ur + unit[:F], ui
     w2r, w2i = ur + result[2 * F:3 * F], ui + result[3 * F:]
@@ -449,27 +504,28 @@
     both = rows(lanes(ends, zero), lanes(zero, ends))
     packed = mmt(left3(packed), right3(both))
 
-    @pl.when(slab < slabs - 1)
-    def _():
-        send_ref[...] = packed
+    send_ref[...] = packed
+
+    @pl.when(slab < last)
+    def _():
         forward.start()
 
-    @pl.when(slab == slabs - 1)
-    def _():
-        send_back_ref[...] = packed
-        backward.start()
-
-    lhs_ref[3, :width, :] = lanes(left3(sym + skew), left3(sym - skew))
-    first_g = lhs_ref[0, :width, :]
-    part_g = first_g[:, :width].astype(f32) + first_g[:, 2 * width:3 * width].astype(f32) + unit
-    part_t = first_g[:, 3 * width:4 * width].astype(f32) + first_g[:, 5 * width:].astype(f32) + unit
+    @pl.when(slab == last)
+    def _():
+        for t in (3, 2, 4, 1, 5, 0, 6):
+            messages[t].start()
+
+    put(g_ref.at[3], sym + skew)
+    put(t_ref.at[3], sym - skew)
+    part_g = g_ref[0, 0].astype(f32) + g_ref[0, 1].astype(f32) + unit
+    part_t = t_ref[0, 0].astype(f32) + t_ref[0, 1].astype(f32) + unit
     for level in range(1, 4):
-        part_g = part_g + mm(lanes(left3(part_g), left3(part_t)), w_ref[level])
+        part_g = part_g + mm(lanes(left3(part_g), left3(part_t)), as_weights(s_ref.at[level], k_ref.at[level]))
         part_t = part_g.T
-    grown = mm(lhs_ref[3, :width, :], w_ref[3])
+    grown = mm(lanes(tripled(g_ref.at[3]), tripled(t_ref.at[3])), as_weights(s_ref.at[3], k_ref.at[3]))
     flipped = grown.T
-    last = rows(right3v(0.5 * (grown + flipped)), right3v(0.5 * (grown - flipped)))
-    part_g = part_g + mm(lanes(left3(part_g), left3(part_t)), last)
+    highest = rows(right3v(0.5 * (grown + flipped)), right3v(0.5 * (grown - flipped)))
+    part_g = part_g + mm(lanes(left3(part_g), left3(part_t)), highest)
     part_t = part_g.T
     pr = 0.5 * (part_g + part_t)
     pi = 0.5 * (part_g - part_t)
@@ -479,6 +535,12 @@
     right = rows(right3v(lanes(pr, pi)), right3v(lanes(pi, -pr)))
     block = scale * mm(left, right)
     block_face = lanes(block[:F, :F], block[:F, width:width + F])
+    face_all[slab] = block_face
+    for t in (2, 1, 3, 0, 4, 5):
+        @pl.when(face_goes(t))
+        def _():
+            give_face[t].start()
+
     hr, qr = split(block[:, :width])
     hi, qi = split(block[:, width:])
     turned = mm(perm_t_ref[...], lanes(hr, qr, hi, qi))
@@ -487,11 +549,11 @@
     x_ref[0] = back[:width] + back[width:2 * width]
     x_ref[1] = back[2 * width:3 * width] + back[3 * width:]
 
-    @pl.when(slab == slabs - 1)
+    @pl.when(slab == last)
     def _():
         out_ref[0, 0, :, :, :] = x_ref[...]
 
-    @pl.when(slab < slabs - 1)
+    @pl.when(slab < last)
     def _():
         column = left3(
             lanes(
@@ -502,31 +564,61 @@
         face_rows = mm(rows(hr[:F], qr[:F], hi[:F], qi[:F]), perm)
         rr = face_rows[:F] + face_rows[F:2 * F]
         ri = face_rows[2 * F:3 * F] + face_rows[3 * F:]
-        across = right3v(rows(lanes(rr, ri), lanes(-ri, rr)))
-        d = d_ref[...]
-        d_both = right3(rows(lanes(d, zero), lanes(zero, d)))
-        u = left3(mm(left3(d), right3v(block_face)))
-        v = right3v(as_right(mmt(left3(block_face), d_both)))
-        k = mmt(u, d_both)
-        backward.wait_recv()
+        across = across_of(rr, ri)
+        one = unit[:F, :2 * F]
+        part_ref[0] = jnp.zeros((F, 2 * F), f32)
+        part_ref[1] = one
+        part_ref[2] = one
+
+        def compose(t, carry):
+            remote(face_all.at[t], face_all.at[t], spread_sem.at[2, 0], face_sem.at[t], slab=slab).wait_recv()
+            g = face_all[t]
+            d = d_all[t - 1]
+            both = right3(rows(lanes(d, zero), lanes(zero, d)))
+            u = mm(left3(d), right3v(g))
+            v = mmt(left3(g), both)
+            k = mmt(left3(u), both)
+            before, behind = part_ref[1], right3v(as_right(part_ref[2]))
+            before = left3(before)
+            part_ref[0] += mm(left3(mm(before, right3v(as_right(k)))), behind)
+            part_ref[1] = mm(before, right3v(as_right(u)))
+            part_ref[2] = mm(left3(v), behind)
+            return carry
+
+        lax.fori_loop(slab + 1, last, compose, 0)
+        wide = mm(column, lanes(right3v(as_right(part_ref[0])), right3v(as_right(part_ref[1]))))
+        more = mm(left3(wide[:, :2 * F]), across)
+        x_ref[0] += more[:, :width]
+        x_ref[1] += more[:, width:]
+        column = left3(wide[:, 2 * F:])
+        across = mm(left3(part_ref[2]), across_of(rr, ri))
+        rr, ri = across[:, :width], across[:, width:]
+        across = across_of(rr, ri)
+        messages[0].wait_recv()
         incoming = right3v(as_right(m_ref[...]))
-
-        @pl.when(slab > 0)
-        def _():
-            send_back_ref[...] = k + mm(left3(mm(u, incoming)), v)
-            backward.start()
-
         more = mm(left3(mm(column, incoming)), across)
         out_ref[0, 0, 0, :, :] = x_ref[0] + more[:, :width]
         out_ref[0, 0, 1, :, :] = x_ref[1] + more[:, width:]
 
-    @pl.when(slab < slabs - 1)
+    @pl.when(slab < last)
     def _():
         forward.wait_send()
 
-    @pl.when(slab > 0)
-    def _():
-        backward.wait_send()
+    @pl.when(slab == last)
+    def _():
+        for t in range(last):
+            messages[t].wait_send()
+
+    for t in range(slabs):
+        @pl.when(d_goes(t))
+        def _():
+            give_d[t].wait_send()
+
+        if t < last:
+            @pl.when(face_goes(t))
+            def _():
+                give_face[t].wait_send()
+
     settle()
 
 
@@ -544,16 +636,27 @@
         scratch_shapes=EXCHANGE_SCRATCH(width) + [
             pltpu.VMEM((width, width), bf16),
             pltpu.VMEM((width, width), bf16),
-            face_block, face_block, face_block, face_block, face_block,
+            face_block,
+            pltpu.VMEM((faces, faces), bf16),
+            pltpu.VMEM((slabs, faces, faces), f32),
+            pltpu.VMEM((slabs, faces, 2 * faces), f32),
+            face_block, face_block,
             pltpu.VMEM((2 * width, width), f32),
-            pltpu.VMEM((4, width + 2 * faces, 6 * width), bf16),
-            pltpu.VMEM((4, 6 * width, width), bf16),
+            pltpu.VMEM((4, 2, width, width), bf16),
+            pltpu.VMEM((4, 2, width, width), bf16),
+            pltpu.VMEM((4, 2, width, width), bf16),
+            pltpu.VMEM((4, 2, width, width), bf16),
+            pltpu.VMEM((2, 2, 2 * faces, width), bf16),
             pltpu.VMEM((width, 2 * width), f32),
-            face_pair, face_pair, face_pair, face_pair,
+            face_pair, face_pair, face_pair,
+            pltpu.VMEM((3, faces, 2 * faces), f32),
             pltpu.VMEM((width, 2 * faces), f32),
             pltpu.VMEM((2, width, width), f32),
-            pltpu.SemaphoreType.DMA((4,)),
-            pltpu.SemaphoreType.DMA((4,)),
+            pltpu.SemaphoreType.DMA((2,)),
+            pltpu.SemaphoreType.DMA((3,)),
+            pltpu.SemaphoreType.DMA((3, slabs)),
+            pltpu.SemaphoreType.DMA((slabs,)),
+            pltpu.SemaphoreType.DMA((slabs,)),
         ],
         compiler_params=pltpu.CompilerParams(
             collective_id=0, has_side_effects=True, vmem_limit_bytes=48 * 1024 * 1024

time: 135 us -> 102 us (0.76)
  the two profiles are of different devices: /device:TPU:6 before, /device:TPU:64 now
where the time goes in v3:
time: 102 us
  Pallas kernels  96.1 us (94%)
  local copies, waits for them, and re-layouts  5.17 us (5%)
    pallas_call x1, Pallas kernels, run(): pl.pallas_call(functools.partial(born_kernel, lines, slabs, width, faces)...  96.1 us
    unnamed x19, local copies, waits for them, and re-layouts  5.17 us

profile of v3, /device:TPU:64, one launch (start us, length us, event | category | flops | bytes accessed | tf_op | source)
XLA Modules:
  0.0 102.0 jit_solution(9087258247333406152)
XLA Ops:
  0.7 0.0 copy-start.7
  0.7 0.0 copy-start.8
  0.7 0.0 copy-start.4
  0.7 0.0 copy-start.5
  0.7 0.0 copy-start.6
  0.7 0.6 copy-done.7
  1.3 0.0 copy-done.8
  1.3 0.0 copy-done.4
  1.3 0.0 copy-done.5
  1.4 0.0 copy-done.6
  1.4 0.0 copy-start
  1.4 1.0 %copy-done = f32[1,1,2,256,256]{4,3,2,1,0:T(8,128)S(1)} copy-done((f32[1,1,2,256,256]{4,3,2,1,0:T(8,128)S(1)}, f32[1,1,2,256,256]{4,3,2,1,0:T(8,128)}, u32[]{:S(2)}) %copy-start) | copy-done | bytes 524312
  2.4 0.0 copy-start.1
  2.4 0.9 copy-done.1
  3.4 0.0 copy-start.2
  3.4 0.9 copy-done.2
  4.3 0.0 copy-start.3
  4.3 0.8 copy-done.3
  5.1 96.1 %born.1 = f32[1,1,2,256,256]{4,3,2,1,0:T(8,128)S(1)} custom-call(f32[1,1]{1,0:T(1,128)} %bitcast.4.energy_ref, s32[1,2]{1,0:T(1,128)S(1)} %copy-done.4, s32[1,2]{1,0:T(1,128)S(1)} %copy-done.5, f32[8]{0:T(128)S(1)} %copy-done.6, f32[512,256]{1,0:T(8,128)S(1)} %bitcast.5, f32[256,256]{1,0:T(8,128)S(1)} %bitcast.6, f32[256,256]{1,0:T(8,128)S(1)} %copy-done.2, ...), custom_call_target="tpu_custom_call" | custom-call | tf_op jit(solution)/shard_map/born/pallas_call | solution.py:631
  101.2 0.8 copy.13
Async XLA Ops:
  0.7 0.7 copy-start.7
  0.7 0.7 copy-start.8
  0.7 0.7 copy-start.4
  0.7 0.7 copy-start.5
  0.7 0.7 copy-start.6
  1.4 1.0 %copy-start = (f32[1,1,2,256,256]{4,3,2,1,0:T(8,128)S(1)}, f32[1,1,2,256,256]{4,3,2,1,0:T(8,128)}, u32[]{:S(2)}) copy-start(f32[1,1,2,256,256]{4,3,2,1,0:T(8,128)} %param.13) | copy-start | bytes 1572868
  2.4 0.9 copy-start.1
  3.4 0.9 copy-start.2
  4.3 0.8 copy-start.3

commit v4 on v3

--- a/solution.py
+++ b/solution.py
@@ -79,11 +79,13 @@
 
 NX = 4
 CORES = 2
-CHUNKS = 8
+DEPTHS = (64,) * 8
+CHUNKS = len(DEPTHS)
 AHEAD = 3
 FAR_LAG = 2
 PARTNER_LAG = 3
 LINE_LAG = 5
+MEANWHILE = (1, 2, 3, 6)
 TABLE = 32
 
 
@@ -123,9 +125,9 @@
         count = count + 2 * there.astype(jnp.int32)
     if slabs > 1:
         slab = lax.axis_index("slab")
-        for step in range(1, slabs):
+        for step in (1, slabs - 1):
             signal(slab=lax.rem(slab + step, slabs))
-        count = count + slabs - 1
+        count = count + 2
     return barrier, count
 
 
@@ -140,10 +142,10 @@
     table_ref[0] = total
 
 
-def exchange(lines, own, table_ref, got, part_send, part_recv, line_send, line_recv, acc,
+def exchange(lines, green, own, table_ref, got, part_send, part_recv, line_send, line_recv, acc,
              send_sem, recv_sem, table_send, table_recv, meanwhile, finish):
     x, z, core = where_on_energy()
-    depth = own.shape[0] // CHUNKS
+    starts = [sum(DEPTHS[:q]) for q in range(CHUNKS)]
     right = energy_of(lax.rem(x + 1, NX), z, core)
     left = energy_of(lax.rem(x + NX - 1, NX), z, core)
     partner = energy_of(x, z, 1 - core)
@@ -151,8 +153,11 @@
     up, down = energy_of(x, z + 1, core), energy_of(x, z - 1, core)
     up_other, down_other = energy_of(x, z + 1, 1 - core), energy_of(x, z - 1, 1 - core)
 
+    def span(chunk):
+        return pl.ds(starts[chunk], DEPTHS[chunk])
+
     def part(ref, chunk):
-        return ref.at[pl.ds(chunk * depth, depth), :]
+        return ref.at[span(chunk), :]
 
     def tables(flow, device):
         return remote(table_ref.at[0], table_ref.at[flow + 1], table_send.at[flow], table_recv.at[flow], energy=device)
@@ -164,8 +169,8 @@
     def piece(flow, chunk, source, target, device):
         return remote(source, target, send_sem.at[flow, chunk], recv_sem.at[flow, chunk], energy=device)
 
-    to_right = [piece(0, q, part(own, q), part(got.at[0], q), right) for q in range(CHUNKS)]
-    to_left = [piece(1, q, part(own, q), part(got.at[1], q), left) for q in range(CHUNKS)]
+    to_right = [piece(0, q, part(green, q), part(got.at[0], q), right) for q in range(CHUNKS)]
+    to_left = [piece(1, q, part(green, q), part(got.at[1], q), left) for q in range(CHUNKS)]
     onward = [
         piece(2, q, part(got.at[q % 2], q), part(got.at[2], q), right if q % 2 == 0 else left)
         for q in range(CHUNKS)
@@ -219,7 +224,7 @@
         for k in range(4):
             lag = 2 * apart[k] + (2 * core - 1 if other else 0) - 8 * line + TABLE // 2
             weight = table_ref[slot, pl.ds(lag, 1), :]
-            block = (own if k == 0 else got.at[k - 1])[pl.ds(chunk * depth, depth), :]
+            block = (own if k == 0 else got.at[k - 1])[span(chunk), :]
             term = lanes(weight, weight) * block
             total = term if total is None else total + term
         return total
@@ -232,12 +237,12 @@
             onward[q].start()
             if q + AHEAD < CHUNKS:
                 own_start(q + AHEAD)
-        if step in (1, 3):
-            meanwhile[(step + 1) // 2]()
+        if step in MEANWHILE:
+            meanwhile[1 + MEANWHILE.index(step)]()
         q = step - FAR_LAG
         if 0 <= q < CHUNKS:
             onward[q].wait_recv()
-            piece_rows = pl.ds(q * depth, depth)
+            piece_rows = span(q)
             acc[piece_rows, :] = weighted(0, 0, False, q)
             part_send[0, piece_rows, :] = weighted(1, 0, True, q)
             across[0][q].start()
@@ -255,7 +260,7 @@
                 across[2][q].start()
         q = step - PARTNER_LAG
         if 0 <= q < CHUNKS:
-            piece_rows = pl.ds(q * depth, depth)
+            piece_rows = span(q)
             across[0][q].wait_recv()
             acc[piece_rows, :] += part_recv[0, piece_rows, :]
 
@@ -272,7 +277,7 @@
                 downward[q].start()
         q = step - LINE_LAG
         if 0 <= q < CHUNKS:
-            piece_rows = pl.ds(q * depth, depth)
+            piece_rows = span(q)
 
             @pl.when(down_there)
             def _():
@@ -284,7 +289,7 @@
                 downward[q].wait_recv()
                 acc[piece_rows, :] += line_recv[1, piece_rows, :]
 
-            finish(q, depth)
+            finish(starts[q], DEPTHS[q])
 
     def settle():
         for q in range(CHUNKS):
@@ -323,12 +328,13 @@
 
 def born_kernel(
     lines, slabs, width, faces,
-    energy_ref, source_ref, index_ref, weights_ref, green_ref, ham_ref, profile_ref, coup_ref, left_ref, right_ref,
+    energy_ref, source_ref, index_ref, weights_ref, green_in, ham_in, profile_in, coup_in, left_in, right_in,
     out_ref,
+    green_ref, ham_ref, profile_ref, coup_ref, left_ref, right_ref, load_sem,
     table_ref, got, part_send, part_recv, line_send, line_recv, acc, piece_send, piece_recv, table_send, table_recv,
     perm_ref, perm_t_ref, next_ref, order_ref, d_all, face_all, ends_ref, lead_ref,
     sk_ref, g_ref, t_ref, s_ref, k_ref, thin_ref, a_ref, b_ref, m_ref, send_ref, part_ref, pa_ref, x_ref,
-    send_sem, recv_sem, spread_sem, d_sem, face_sem,
+    send_sem, recv_sem, spread_sem, d_sem, face_sem, known_sem,
 ):
     slab = lax.axis_index("slab")
     F = faces
@@ -336,6 +342,15 @@
     col = lax.broadcasted_iota(jnp.int32, (width, width), 1)
     unit = jnp.where(row == col, 1.0, 0.0)
     barrier, greetings = greet(lines, slabs)
+    loads = [
+        pltpu.make_async_copy(source, target, load_sem.at[k])
+        for k, (source, target) in enumerate((
+            (coup_in, coup_ref), (left_in, left_ref), (right_in, right_ref),
+            (green_in, green_ref), (ham_in, ham_ref), (profile_in, profile_ref),
+        ))
+    ]
+    for load in loads:
+        load.start()
     make_table(source_ref, index_ref, weights_ref, table_ref)
     pl.semaphore_wait(barrier, greetings)
     last = slabs - 1
@@ -358,7 +373,16 @@
 
     zero = jnp.zeros((F, F), f32)
 
+    def tell(hop):
+        for step in (1, last):
+            pl.semaphore_signal(
+                known_sem.at[hop], inc=1, device_id={"slab": lax.rem(slab + step, slabs)}, device_id_type=MESH
+            )
+
     def first_stage():
+        tell(0)
+        for load in loads:
+            load.wait()
         give_coupling.start()
         spot = lax.broadcasted_iota(jnp.int32, (width, F), 0)
         hot_left = jnp.where(spot == left_ref[...], 1.0, 0.0)
@@ -374,7 +398,13 @@
         coup = coup_ref[...]
         lead_ref[...] = -0.5 * mm(left3(coup.T), right3v(coup))
 
+    def hear_stage():
+        pl.semaphore_wait(known_sem.at[0], 2)
+        tell(1)
+
     def second_stage():
+        pl.semaphore_wait(known_sem.at[1], 2)
+        tell(2)
         give_coupling.wait()
         following = next_ref[...]
         high, low = split(following)
@@ -383,6 +413,9 @@
         here = mm(lanes(order, order, order), rows(high, low, lowest))
         d_all[slab] = here
         ends_ref[...] = here.T
+
+    def spread_stage():
+        pl.semaphore_wait(known_sem.at[2], 2)
         for t in range(slabs):
             @pl.when(d_goes(t))
             def _():
@@ -400,9 +433,8 @@
             arrived(last - 1, 0)
             ends_ref[...] = d_all[last - 1]
 
-    def finish(chunk, depth):
-        piece_rows = pl.ds(chunk * depth, depth)
-        first = chunk * depth
+    def finish(first, depth):
+        piece_rows = pl.ds(first, depth)
         imag = first >= width
         there = pl.ds(first - width if imag else first, depth)
         diagonal = jnp.where(
@@ -414,11 +446,11 @@
         if imag:
             acc[piece_rows, :] = BROAD * diagonal - sigma
         else:
-            acc[piece_rows, :] = energy_ref[...] * diagonal - ham_ref[there, :] - sigma
-
-    settle = exchange(lines, green_ref, table_ref, got, part_send, part_recv, line_send, line_recv, acc,
+            acc[piece_rows, :] = energy_ref[0] * diagonal - ham_ref[there, :] - sigma
+
+    settle = exchange(lines, green_in, green_ref, table_ref, got, part_send, part_recv, line_send, line_recv, acc,
                       piece_send, piece_recv, table_send, table_recv,
-                      (first_stage, second_stage, third_stage), finish)
+                      (first_stage, hear_stage, second_stage, spread_stage, third_stage), finish)
 
     perm = perm_ref[...]
     pieces = split(acc[:width, :]) + split(acc[width:, :])
@@ -631,9 +663,17 @@
     return pl.pallas_call(
         functools.partial(born_kernel, lines, slabs, width, faces),
         out_shape=jax.ShapeDtypeStruct((1, 1, 2, width, width), f32),
-        in_specs=[vmem, smem, smem, smem] + [vmem] * 6,
+        in_specs=[smem] * 4 + [pl.BlockSpec(memory_space=pltpu.HBM)] * 6,
         out_specs=vmem,
-        scratch_shapes=EXCHANGE_SCRATCH(width) + [
+        scratch_shapes=[
+            pltpu.VMEM((2 * width, width), f32),
+            pltpu.VMEM((width, width), f32),
+            pltpu.VMEM((width, width), f32),
+            face_block,
+            pltpu.VMEM((1, faces), jnp.int32),
+            pltpu.VMEM((1, faces), jnp.int32),
+            pltpu.SemaphoreType.DMA((6,)),
+        ] + EXCHANGE_SCRATCH(width) + [
             pltpu.VMEM((width, width), bf16),
             pltpu.VMEM((width, width), bf16),
             face_block,
@@ -657,13 +697,14 @@
             pltpu.SemaphoreType.DMA((3, slabs)),
             pltpu.SemaphoreType.DMA((slabs,)),
             pltpu.SemaphoreType.DMA((slabs,)),
+            pltpu.SemaphoreType.REGULAR((3,)),
         ],
         compiler_params=pltpu.CompilerParams(
-            collective_id=0, has_side_effects=True, vmem_limit_bytes=48 * 1024 * 1024
+            collective_id=0, has_side_effects=True, vmem_limit_bytes=67043328
         ),
         name="born",
     )(
-        energies.reshape(1, 1), source, weight_index, phonon_weights,
+        energies, source, weight_index, phonon_weights,
         green_prev.reshape(2 * width, width), hamiltonian[0], profile, coupling[0], left, right,
     )
 

time: 102 us -> 97.3 us (0.954)
  the two profiles are of different devices: /device:TPU:64 before, /device:TPU:6 now
where the time goes in v4:
time: 97.3 us; the launch traced here: 95.5 us
  Pallas kernels  93 us (96%)
  local copies, waits for them, and re-layouts  1.87 us (2%)
    pallas_call x1, Pallas kernels, run(): pl.pallas_call(functools.partial(born_kernel, lines, slabs, width, faces)...  93 us

profile of v4, /device:TPU:6, one launch (start us, length us, event | category | flops | bytes accessed | tf_op | source)
XLA Modules:
  0.0 95.5 jit_solution(16653010288969439234)
XLA Ops:
  0.7 93.0 %born.1 = f32[1,1,2,256,256]{4,3,2,1,0:T(8,128)} custom-call(f32[1]{0:T(128)S(6)} %copy.12.energy_ref, s32[1,2]{1,0:T(1,128)} %source_ref.1, s32[1,2]{1,0:T(1,128)} %index_ref.1, f32[8]{0:T(128)} %weights_ref.1, f32[512,256]{1,0:T(8,128)} %bitcast.3, f32[256,256]{1,0:T(8,128)} %bitcast.4, f32[256,256]{1,0:T(8,128)} %profile_in.1, f32[64,64]{1,0:T(8,128)} %bitcast.5, ...), custom_call_target="tpu_custom_call" | custom-call | tf_op jit(solution)/shard_map/born/pallas_call | solution.py:663
  93.7 1.9 %copy.13 = f32[1,1,2,256,256]{4,3,2,1,0:T(8,128)} copy(f32[1,1,2,256,256]{4,3,2,1,0:T(8,128)} %born.1) | data formatting | bytes 1048576

commit v5 on v4

--- a/solution.py
+++ b/solution.py
@@ -86,6 +86,7 @@
 PARTNER_LAG = 3
 LINE_LAG = 5
 MEANWHILE = (1, 2, 3, 6)
+FACTORS = (1.0, 2.0, 4.0, 16.0)
 TABLE = 32
 
 
@@ -507,27 +508,36 @@
     lr = scale * over[2 * F:3 * F]
     li = scale * over[3 * F:]
 
+    def thin(level, real, imag):
+        put(thin_ref.at[0], rows(real, imag))
+        put(thin_ref.at[1], rows(-imag, real))
+        product = mm(
+            lanes(tripled(thin_ref.at[0]), tripled(thin_ref.at[1])), as_weights(s_ref.at[level], k_ref.at[level])
+        )
+        return product * (1.0 / FACTORS[level])
+
+    grown, flipped = sym + skew, sym - skew
     for level in range(3):
         put(s_ref.at[level], sym)
         put(k_ref.at[level], skew)
-        put(g_ref.at[level], sym + skew)
-        put(t_ref.at[level], sym - skew)
-        put(thin_ref.at[0], rows(lr, li))
-        put(thin_ref.at[1], rows(-li, lr))
-        weights = as_weights(s_ref.at[level], k_ref.at[level])
-        grown = mm(lanes(tripled(g_ref.at[level]), tripled(t_ref.at[level])), weights)
-        flipped = grown.T
-        sym = 0.5 * (grown + flipped)
-        skew = 0.5 * (grown - flipped)
-        result = mm(lanes(tripled(thin_ref.at[0]), tripled(thin_ref.at[1])), weights)
+        put(g_ref.at[level], grown)
+        put(t_ref.at[level], flipped)
+        grown = mm(
+            lanes(tripled(g_ref.at[level]), tripled(t_ref.at[level])), as_weights(s_ref.at[level], k_ref.at[level])
+        )
+        result = thin(level, lr, li)
         lr = lr + result[:F]
         li = li + result[F:]
+        flipped = grown.T
+        sym = grown + flipped
+        skew = grown - flipped
     put(s_ref.at[3], sym)
     put(k_ref.at[3], skew)
-    ur, ui = sym[:F], skew[:F]
-    result = mm(
-        lanes(left3(rows(lr, li, ur, ui)), left3(rows(-li, lr, -ui, ur))), as_weights(s_ref.at[3], k_ref.at[3])
-    )
+    ur, ui = sym[:F] * (1.0 / FACTORS[3]), skew[:F] * (1.0 / FACTORS[3])
+    upper = mm(
+        lanes(left3(rows(ur, ui)), left3(rows(-ui, ur))), as_weights(s_ref.at[3], k_ref.at[3])
+    ) * (1.0 / FACTORS[3])
+    result = rows(thin(3, lr, li), upper)
     w1r, w1i = ur + unit[:F], ui
     w2r, w2i = ur + result[2 * F:3 * F], ui + result[3 * F:]
     left = left3(lanes(lr, li, result[:F], result[F:2 * F]))
@@ -547,16 +557,19 @@
         for t in (3, 2, 4, 1, 5, 0, 6):
             messages[t].start()
 
-    put(g_ref.at[3], sym + skew)
-    put(t_ref.at[3], sym - skew)
+    put(g_ref.at[3], grown)
+    put(t_ref.at[3], flipped)
     part_g = g_ref[0, 0].astype(f32) + g_ref[0, 1].astype(f32) + unit
     part_t = t_ref[0, 0].astype(f32) + t_ref[0, 1].astype(f32) + unit
     for level in range(1, 4):
-        part_g = part_g + mm(lanes(left3(part_g), left3(part_t)), as_weights(s_ref.at[level], k_ref.at[level]))
+        part_g = part_g + mm(lanes(left3(part_g), left3(part_t)), as_weights(s_ref.at[level], k_ref.at[level])) * (
+            1.0 / FACTORS[level]
+        )
         part_t = part_g.T
     grown = mm(lanes(tripled(g_ref.at[3]), tripled(t_ref.at[3])), as_weights(s_ref.at[3], k_ref.at[3]))
     flipped = grown.T
-    highest = rows(right3v(0.5 * (grown + flipped)), right3v(0.5 * (grown - flipped)))
+    half = 0.5 * FACTORS[1] / (FACTORS[3] * FACTORS[3])
+    highest = rows(right3v(half * (grown + flipped)), right3v(half * (grown - flipped)))
     part_g = part_g + mm(lanes(left3(part_g), left3(part_t)), highest)
     part_t = part_g.T
     pr = 0.5 * (part_g + part_t)

time: 97.3 us -> 94.6 us (0.972)
  Pallas kernels: 93 us -> 90.2 us
    pallas_call x1, Pallas kernels: 93 us -> 90.2 us  [run(): pl.pallas_call(functools.partial(born_kernel, lines, slabs, width, faces)...]
where the time goes in v5:
time: 94.6 us; the launch traced here: 92.8 us
  Pallas kernels  90.2 us (95%)
  local copies, waits for them, and re-layouts  1.87 us (2%)
    pallas_call x1, Pallas kernels, run(): pl.pallas_call(functools.partial(born_kernel, lines, slabs, width, faces)...  90.2 us

profile of v5, /device:TPU:6, one launch (start us, length us, event | category | flops | bytes accessed | tf_op | source)
XLA Modules:
  0.0 92.8 jit_solution(403242149045707193)
XLA Ops:
  0.7 90.2 %born.1 = f32[1,1,2,256,256]{4,3,2,1,0:T(8,128)} custom-call(f32[1]{0:T(128)S(6)} %copy.12.energy_ref, s32[1,2]{1,0:T(1,128)} %source_ref.1, s32[1,2]{1,0:T(1,128)} %index_ref.1, f32[8]{0:T(128)} %weights_ref.1, f32[512,256]{1,0:T(8,128)} %bitcast.3, f32[256,256]{1,0:T(8,128)} %bitcast.4, f32[256,256]{1,0:T(8,128)} %profile_in.1, f32[64,64]{1,0:T(8,128)} %bitcast.5, ...), custom_call_target="tpu_custom_call" | custom-call | tf_op jit(solution)/shard_map/born/pallas_call | solution.py:676
  90.9 1.9 %copy.13 = f32[1,1,2,256,256]{4,3,2,1,0:T(8,128)} copy(f32[1,1,2,256,256]{4,3,2,1,0:T(8,128)} %born.1) | data formatting | bytes 1048576

commit v6 on v5

--- a/solution.py
+++ b/solution.py
@@ -18,6 +18,11 @@
 
 def mmt(left, right):
     return lax.dot_general(left, right, (((1,), (1,)), ((), ())), preferred_element_type=f32)
+
+
+def by_halves(left, right):
+    half = left.shape[0] // 2
+    return rows(mm(left[:half], right), mm(left[half:], right))
 
 
 def split(value):
@@ -522,7 +527,7 @@
         put(k_ref.at[level], skew)
         put(g_ref.at[level], grown)
         put(t_ref.at[level], flipped)
-        grown = mm(
+        grown = by_halves(
             lanes(tripled(g_ref.at[level]), tripled(t_ref.at[level])), as_weights(s_ref.at[level], k_ref.at[level])
         )
         result = thin(level, lr, li)
@@ -562,15 +567,15 @@
     part_g = g_ref[0, 0].astype(f32) + g_ref[0, 1].astype(f32) + unit
     part_t = t_ref[0, 0].astype(f32) + t_ref[0, 1].astype(f32) + unit
     for level in range(1, 4):
-        part_g = part_g + mm(lanes(left3(part_g), left3(part_t)), as_weights(s_ref.at[level], k_ref.at[level])) * (
+        part_g = part_g + by_halves(lanes(left3(part_g), left3(part_t)), as_weights(s_ref.at[level], k_ref.at[level])) * (
             1.0 / FACTORS[level]
         )
         part_t = part_g.T
-    grown = mm(lanes(tripled(g_ref.at[3]), tripled(t_ref.at[3])), as_weights(s_ref.at[3], k_ref.at[3]))
+    grown = by_halves(lanes(tripled(g_ref.at[3]), tripled(t_ref.at[3])), as_weights(s_ref.at[3], k_ref.at[3]))
     flipped = grown.T
     half = 0.5 * FACTORS[1] / (FACTORS[3] * FACTORS[3])
     highest = rows(right3v(half * (grown + flipped)), right3v(half * (grown - flipped)))
-    part_g = part_g + mm(lanes(left3(part_g), left3(part_t)), highest)
+    part_g = part_g + by_halves(lanes(left3(part_g), left3(part_t)), highest)
     part_t = part_g.T
     pr = 0.5 * (part_g + part_t)
     pi = 0.5 * (part_g - part_t)

time: 94.6 us -> 92.6 us (0.979)
  Pallas kernels: 90.2 us -> 88.3 us
    pallas_call x1, Pallas kernels: 90.2 us -> 88.3 us  [run(): pl.pallas_call(functools.partial(born_kernel, lines, slabs, width, faces)...]
where the time goes in v6:
time: 92.6 us; the launch traced here: 90.8 us
  Pallas kernels  88.3 us (95%)
  local copies, waits for them, and re-layouts  1.87 us (2%)
    pallas_call x1, Pallas kernels, run(): pl.pallas_call(functools.partial(born_kernel, lines, slabs, width, faces)...  88.3 us
    unnamed x1, local copies, waits for them, and re-layouts  1.87 us

profile of v6, /device:TPU:6, one launch (start us, length us, event | category | flops | bytes accessed | tf_op | source)
XLA Modules:
  0.0 90.8 jit_solution(11247200502301070406)
XLA Ops:
  0.7 88.3 %born.1 = f32[1,1,2,256,256]{4,3,2,1,0:T(8,128)} custom-call(f32[1]{0:T(128)S(6)} %copy.12.energy_ref, s32[1,2]{1,0:T(1,128)} %source_ref.1, s32[1,2]{1,0:T(1,128)} %index_ref.1, f32[8]{0:T(128)} %weights_ref.1, f32[512,256]{1,0:T(8,128)} %bitcast.3, f32[256,256]{1,0:T(8,128)} %bitcast.4, f32[256,256]{1,0:T(8,128)} %profile_in.1, f32[64,64]{1,0:T(8,128)} %bitcast.5, ...), custom_call_target="tpu_custom_call" | custom-call | tf_op jit(solution)/shard_map/born/pallas_call | solution.py:681
  88.9 1.9 %copy.13 = f32[1,1,2,256,256]{4,3,2,1,0:T(8,128)} copy(f32[1,1,2,256,256]{4,3,2,1,0:T(8,128)} %born.1) | data formatting | bytes 1048576

commit v7 on v6

--- a/solution.py
+++ b/solution.py
@@ -88,7 +88,7 @@
 CHUNKS = len(DEPTHS)
 AHEAD = 3
 FAR_LAG = 2
-PARTNER_LAG = 3
+PARTNER_LAG = 2
 LINE_LAG = 5
 MEANWHILE = (1, 2, 3, 6)
 FACTORS = (1.0, 2.0, 4.0, 16.0)
@@ -476,7 +476,9 @@
     rh, rl = split(open_real)
     ih, il = split(open_imag)
     left = rows(lanes(rh, rh, rl, ih, ih, il), lanes(ih, ih, il, -rh, -rh, -rl))
-    sk_ref[...] = mmt(left, lanes(rh, rl, rh, ih, il, ih))
+    right = lanes(rh, rl, rh, ih, il, ih)
+    sk_ref[:width, :] = mmt(left[:width], right)
+    sk_ref[width:, :] = mmt(left[width:], right)
 
     @pl.when(slab == 0)
     def _():

time: 92.6 us -> 89.5 us (0.967)
  Pallas kernels: 88.3 us -> 85.5 us
    pallas_call x1, Pallas kernels: 88.3 us -> 85.5 us  [run(): pl.pallas_call(functools.partial(born_kernel, lines, slabs, width, faces)...]
where the time goes in v7:
time: 89.5 us; the launch traced here: 88.1 us
  Pallas kernels  85.5 us (96%)
  local copies, waits for them, and re-layouts  1.87 us (2%)
    pallas_call x1, Pallas kernels, run(): pl.pallas_call(functools.partial(born_kernel, lines, slabs, width, faces)...  85.5 us
    unnamed x1, local copies, waits for them, and re-layouts  1.87 us

profile of v7, /device:TPU:6, one launch (start us, length us, event | category | flops | bytes accessed | tf_op | source)
XLA Modules:
  0.0 88.1 jit_solution(1704060287521667309)
XLA Ops:
  0.7 85.5 %born.1 = f32[1,1,2,256,256]{4,3,2,1,0:T(8,128)} custom-call(f32[1]{0:T(128)S(6)} %copy.12.energy_ref, s32[1,2]{1,0:T(1,128)} %source_ref.1, s32[1,2]{1,0:T(1,128)} %index_ref.1, f32[8]{0:T(128)} %weights_ref.1, f32[512,256]{1,0:T(8,128)} %bitcast.3, f32[256,256]{1,0:T(8,128)} %bitcast.4, f32[256,256]{1,0:T(8,128)} %profile_in.1, f32[64,64]{1,0:T(8,128)} %bitcast.5, ...), custom_call_target="tpu_custom_call" | custom-call | tf_op jit(solution)/shard_map/born/pallas_call | solution.py:683
  86.2 1.9 %copy.13 = f32[1,1,2,256,256]{4,3,2,1,0:T(8,128)} copy(f32[1,1,2,256,256]{4,3,2,1,0:T(8,128)} %born.1) | data formatting | bytes 1048576
